TPU v7x, 512 devices: a whole 4x4x16 slice. The times are simulated.
512 devices in a mesh: row: 32 (over y_lo, z), col: 16 (over x, y_hi, core).
Axes of the slice: x: 4, y: 4 (y_hi: 2, y_lo: 2; y = y_hi * 2 + y_lo), z: 16, core: 2. Of those that a mesh axis runs over, the one named last changes fastest.
Arguments:
- block_ids: int32 [1024, 8], replicated, may hold values from 0 to 767, as said below
- iface_counts: int32 [1024], replicated, may hold values from 6 to 8
- inv_factor: bfloat16 [483328, 472], P(('row', 'col')), as said below
- coupling: bfloat16 [483328, 1024], P(('row', 'col')), may hold values from -0.375 to 0.375
- boundary_block: bfloat16 [24, 4096, 1, 2048], P(None, 'row', None, 'col'), may hold values from -6 to 6
Outputs:
- schur: float32 [24, 4096, 1, 2048], P(None, 'row', None, 'col')
Inputs may be any that keep to these rules, and one draw needn't show every extreme that they name: For j < 2, block_ids[s, j] is below 16, equals (s // 2 + j) modulo 16, and is the same for the 2 substructures that share s // 2. Apart from these shared first 2 ids, the ids of the 2 substructures that share s // 2 are distinct modulo 32. `inv_factor`: each substructure's block is lower triangular with a diagonal from 0.5 to 1.5.
All inputs are finite; a program needn't handle non-finite values.
Results may differ from a plain program's by a relative error of at most 0.00044.
Values sent between devices are 32-bit elements; how exact they have to be, the bound alone decides.
No kernel may reach another device: no remote copies, remote signals or barrier semaphores. Data moves between devices by JAX's collectives and lax.ppermute only.
A program may use at most 64 MiB of HBM per device.

v0:
```python
import jax
import jax.numpy as jnp
from jax import lax
from jax.sharding import PartitionSpec as P

CS = 2


def passed_along(value, axis, steps):
    count = lax.axis_size(axis)
    pairs = [(source, (source + steps) % count) for source in range(count)]
    return lax.ppermute(value, axis, pairs)


def owner_table(ids, rows):
    return ((ids % rows)[None, :, :] == jnp.arange(rows, dtype=jnp.int32)[:, None, None]).astype(
        jnp.float32
    )


def dispatch(piece, ids, rows):
    return jnp.einsum(
        "psk,skab->pab", owner_table(ids, rows), piece, precision=lax.Precision.HIGHEST
    )


def settle(received, source_ids, column_slot, row_at, rows, cols, nq, cq):
    members = source_ids.shape[1]
    slot_count = source_ids.shape[2]
    single = (jnp.arange(members, dtype=jnp.int32)[:, None] == 0) | (
        jnp.arange(slot_count, dtype=jnp.int32)[None, :] >= CS
    )
    match = (source_ids % rows == row_at) & single[None]
    local_row = jnp.sum(jnp.where(match, source_ids // rows, 0), axis=(1, 2))
    local_col = source_ids[:, 0, column_slot] // cols
    place = (local_row[None, None, :] == jnp.arange(nq, dtype=jnp.int32)[:, None, None]) & (
        local_col[None, None, :] == jnp.arange(cq, dtype=jnp.int32)[None, :, None]
    )
    place = place.reshape(nq * cq, rows).astype(jnp.float32)
    return jnp.dot(place, received.reshape(rows, 128 * 128), precision=lax.Precision.HIGHEST)


def on_device(block_ids, iface_counts, inv_factor, coupling, boundary_block):
    rows = lax.axis_size("row")
    cols = lax.axis_size("col")
    row_at = lax.axis_index("row")
    col_at = lax.axis_index("col")
    slot_count = block_ids.shape[1]
    width = inv_factor.shape[1]
    members = inv_factor.shape[0] // width
    nq = boundary_block.shape[0]
    cq = boundary_block.shape[2]
    grid_ids = block_ids.reshape(rows, cols, members, slot_count)
    grid_counts = iface_counts.reshape(rows, cols, members)
    own_ids = lax.dynamic_index_in_dim(
        lax.dynamic_index_in_dim(grid_ids, row_at, 0, False), col_at, 0, False
    )
    own_count = lax.dynamic_index_in_dim(
        lax.dynamic_index_in_dim(grid_counts, row_at, 0, False), col_at, 0, False
    )
    factors = inv_factor.reshape(members, width, width)
    couples = coupling.reshape(members, width, slot_count * 128)
    tile_list = []
    for member in range(members):
        mixed = jnp.dot(
            factors[member], couples[member], preferred_element_type=jnp.float32
        ).astype(jnp.bfloat16)
        partial_value = lax.dot_general(
            mixed,
            mixed[:, : CS * 128],
            (((0,), (0,)), ((), ())),
            preferred_element_type=jnp.float32,
        )
        live = (jnp.arange(slot_count, dtype=jnp.int32) < own_count[member]).astype(jnp.float32)
        tile_list.append(
            partial_value.reshape(slot_count, 128, CS, 128) * live[:, None, None, None]
        )
    tiles = jnp.stack(tile_list, axis=0)
    sources = [
        lax.dynamic_index_in_dim(grid_ids, (col_at - slot) % cols, 1, False) for slot in range(CS)
    ]
    pieces = []
    outgoing = [dispatch(tiles[:, :, :, 0, :], own_ids, rows)]
    slot = 1
    moved = passed_along(tiles[:, :, :, slot, :], "col", slot)
    moved_ids = lax.dynamic_index_in_dim(sources[slot], row_at, 0, False)
    outgoing.append(dispatch(moved, moved_ids, rows))
    arrived = lax.all_to_all(
        jnp.stack(outgoing, axis=1), "row", split_axis=0, concat_axis=0, tiled=True
    )
    for slot in range(CS):
        pieces.append(arrived[:, slot])
    gathered = settle(pieces[0], sources[0], 0, row_at, rows, cols, nq, cq)
    slot = 1
    gathered = gathered + settle(pieces[slot], sources[slot], slot, row_at, rows, cols, nq, cq)
    gathered = gathered.reshape(nq, cq, 128, 128).transpose(0, 2, 1, 3)
    return boundary_block.astype(jnp.float32) - gathered


def solution(mesh):
    return jax.shard_map(
        on_device,
        mesh=mesh,
        in_specs=(
            P(),
            P(),
            P(("row", "col"), None),
            P(("row", "col"), None),
            P(None, "row", None, "col"),
        ),
        out_specs=P(None, "row", None, "col"),
        check_vma=False,
    )
```

profile of v0, /device:TPU:48, one launch (start us, length us, event | category | flops | bytes accessed | tf_op | source)
XLA Modules:
  0.0 251.1 jit_solution(8205659600210210835)
XLA Ops:
  0.0 2.2 convolution_convert_fusion
  2.2 0.7 convolution_convert_fusion.1
  2.9 0.2 reshape.337
  3.1 0.7 fusion.57
  3.8 0.6 compare_convert_fusion.1
  4.5 0.7 compare_convert_fusion
  5.1 0.5 fusion.17
  5.6 0.5 reshape.338
  6.2 0.5 fusion.19
  6.7 1.5 reshape.336
  8.2 2.4 copy_multiply_fusion
  10.7 1.9 collective-permute-start
  12.7 1.0 copy.31
  13.7 0.7 and_select_fusion.2
  14.4 1.1 convolution_bitcast_fusion.1
  15.5 13.0 %collective-permute-done = f32[2,8,128,128]{3,1,0,2:T(8,128)} collective-permute-done((f32[2,8,128,128]{3,1,0,2:T(8,128)S(1)}, f32[2,8,128,128]{3,1,0,2:T(8,128)}, u32[]{:S(2)}, u32[]{:S(2)}) %collective-permute-start) | collective-permute-done | bytes 1048608 | tf_op jit(solution)/shard_map/ppermute | solution.py:12
  28.4 2.3 convolution_bitcast_fusion
  30.8 0.4 pad_maximum_fusion
  31.2 4.4 %copy.35 = f32[32,2,128,128]{3,2,1,0:T(8,128)} copy(f32[32,2,128,128]{3,0,2,1:T(8,128)S(1)} %pad_maximum_fusion) | data formatting | bytes 8388608 | tf_op jit(solution)/shard_map/stack | solution.py:89
  35.6 16.1 %all-to-all-start = ((f32[32,2,128,128]{3,2,1,0:T(8,128)}), f32[32,2,128,128]{3,2,1,0:T(8,128)}, u32[]{:S(2)}, u32[]{:S(2)}) async-start(f32[32,2,128,128]{3,2,1,0:T(8,128)} %copy.35), calls=%async_computation | async-start | bytes 8388608 | tf_op jit(solution)/shard_map/all_to_all | solution.py:88
  51.8 0.8 constant_dynamic-slice_fusion.4
  52.6 0.1 copy.32
  52.6 0.1 copy.36
  52.7 0.1 broadcast_or_fusion
  52.8 0.1 fusion.32
  52.9 187.3 %all-to-all-done = f32[32,2,128,128]{3,2,1,0:T(8,128)} async-done(((f32[32,2,128,128]{3,2,1,0:T(8,128)}), f32[32,2,128,128]{3,2,1,0:T(8,128)}, u32[]{:S(2)}, u32[]{:S(2)}) %all-to-all-start) | async-done | bytes 4194336 | tf_op jit(solution)/shard_map/all_to_all | solution.py:88
  240.2 2.5 fusion.56
  242.7 2.2 fusion.2
  244.9 2.2 fusion.6
  247.1 0.3 copy.42
  247.4 0.8 copy-done
  248.3 2.9 %fusion.5 = f32[24,128,1,128]{3,2,1,0:T(1,128)} fusion(f32[24,128,1,128]{3,2,1,0:T(1,128)S(1)} %bitcast.80, bf16[24,128,1,128]{3,1,2,0:T(8,128)(2,1)S(1)} %copy-done), kind=kLoop, calls=%fused_computation.12 | loop fusion | flops 786432 | bytes 3932160 | tf_op jit(solution)/shard_map/sub | solution.py:97
  (15 shorter events, 0.2 us)
Async XLA Ops:
  0.0 2.2 copy-start.3
  0.0 2.2 copy-start.4
  2.2 0.7 copy-start.2
  10.6 2.0 copy-start.1
  10.7 17.7 %collective-permute-start = (f32[2,8,128,128]{3,1,0,2:T(8,128)S(1)}, f32[2,8,128,128]{3,1,0,2:T(8,128)}, u32[]{:S(2)}, u32[]{:S(2)}) collective-permute-start(f32[2,8,128,128]{3,1,0,2:T(8,128)S(1)} %fusion.12), channel_id=1, source_target_pairs={{0,1},{1,2},{2,3},{3,4},{4,5},{5,6},{6,7},{7,8},{8,9},{9,10},{10,1... | collective-permute-start | bytes 3145736 | tf_op jit(solution)/shard_map/ppermute | solution.py:12
  35.6 204.6 %all-to-all-start = ((f32[32,2,128,128]{3,2,1,0:T(8,128)}), f32[32,2,128,128]{3,2,1,0:T(8,128)}, u32[]{:S(2)}, u32[]{:S(2)}) async-start(f32[32,2,128,128]{3,2,1,0:T(8,128)} %copy.35), calls=%async_computation | async-start | bytes 8388608 | tf_op jit(solution)/shard_map/all_to_all | solution.py:88
  247.1 1.1 copy-start
where the time goes:
time: 252 us; the launch traced here: 251 us
  waiting for transfers between devices  200 us (79%)
  starting transfers between devices  18.1 us (7%)
  local copies, waits for them, and re-layouts  12.9 us (5%)
  matrix products  11.6 us (5%)
  other arithmetic  8.07 us (3%)
    all_to_all x1, waiting for transfers between devices, on_device(): lax.all_to_all(jnp.stack(outgoing, axis=1), 'row', split_axis=0, concat_a...  187 us
    all_to_all x1, starting transfers between devices, on_device(): lax.all_to_all(jnp.stack(outgoing, axis=1), 'row', split_axis=0, concat_a...  16.1 us
    ppermute x1, waiting for transfers between devices, passed_along(): return lax.ppermute(value, axis, pairs)  13 us
  transfers between devices with their start and end apart: 2, of which 2 were waited for; matrix products, arithmetic and copies ran while one was open for 2% of the time, Pallas kernels for 0%

commit v1 on v0

v1 whole, which is shorter than its diff:
```python
import functools

import jax
import jax.numpy as jnp
from jax import lax
from jax.experimental import pallas as pl
from jax.experimental.pallas import tpu as pltpu
from jax.sharding import Mesh, PartitionSpec as P

CS = 2
YLO, NZ, XS, YHI, CORE = 2, 16, 4, 2, 2
NCOL = XS * YHI * CORE
PLANE = ("ylo", "x", "yhi", "core")
NPLANE = YLO * NCOL
LIVE = 6
SLOTS = 2 * LIVE + CS
NQ = 24
CAP = 36
FULL = 64
TRASH = NPLANE * NQ
VMEM = pl.BlockSpec(memory_space=pltpu.VMEM)
SMEM = pl.BlockSpec(memory_space=pltpu.SMEM)


def low_half(shape):
    return lax.broadcasted_iota(jnp.int32, shape, 0) % 8 < 4


def slice_kernel(first, second, out):
    low = low_half((128, 128))

    def put(slot, left, right):
        even = jnp.where(low, left, jnp.roll(right.reshape(16, 8, 128), 4, axis=1).reshape(128, 128))
        odd = jnp.where(low, jnp.roll(left.reshape(16, 8, 128), 4, axis=1).reshape(128, 128), right)
        even = even.reshape(16, 8, 128)
        odd = odd.reshape(16, 8, 128)
        for i in range(16):
            out[2 * i, slot] = even[i]
            out[2 * i + 1, slot] = odd[i]

    for member, tiles in enumerate((first, second)):
        for k in range(LIVE):
            rows = pl.ds((CS + k) * 128, 128)
            put(member * LIVE + k, tiles[rows, 0:128], tiles[rows, 128:256])
    for k in range(CS):
        rows = pl.ds(k * 128, 128)
        put(
            2 * LIVE + k,
            first[rows, 0:128] + second[rows, 0:128],
            first[rows, 128:256] + second[rows, 128:256],
        )


def pack_kernel(meta, send_list, slices, *outs):
    me = meta[0]
    for d in range(NZ):
        out = outs[d]

        def body(p, carry, d=d, out=out):
            out[p] = slices[send_list[d * CAP + p]]
            return carry

        lax.fori_loop(0, CAP, body, 0, unroll=4)
        target = lax.rem(me + d, NZ)
        for k in range(CS):
            source = lax.rem(target + NZ - k, NZ)
            out[CAP + k] = (
                slices[source * SLOTS + 2 * LIVE + k]
                + slices[(NCOL + source) * SLOTS + 2 * LIVE + k]
            )


def gather_kernel(meta, recv_list, *refs):
    bufs, total = refs[:NZ], refs[NZ]
    me = meta[0]
    total[...] = jnp.zeros_like(total)
    for d in range(NZ):
        buf = bufs[d]
        base = lax.rem(me + NZ - d, NZ) * CAP
        for k in range(CS):
            spot = lax.rem(me + NZ - k, NZ) * NQ
            total[spot] = total[spot] + buf[CAP + k]

        def body(p, carry, base=base, buf=buf):
            spot = recv_list[base + p]
            total[spot] = total[spot] + buf[p]
            return carry

        lax.fori_loop(0, CAP, body, 0, unroll=4)


def rest_pack_kernel(send_list, slices, out):
    def body(p, carry):
        out[p] = slices[send_list[p]]
        return carry

    lax.fori_loop(0, NZ * (FULL - CAP), body, 0)


def rest_gather_kernel(recv_list, buf, before, total):
    total[...] = before[...]

    def body(p, carry):
        spot = recv_list[p]
        total[spot] = total[spot] + buf[p]
        return carry

    lax.fori_loop(0, NZ * (FULL - CAP), body, 0)


def merge_kernel(total, out):
    low = low_half((8, 128))

    def body(at, carry):
        side = at // NCOL * NCOL
        left = lax.rem(at + NCOL - 1, NCOL) + side
        for h in range(NQ // 2):
            a0 = total[at * NQ + 2 * h]
            a1 = total[at * NQ + 2 * h + 1]
            b0 = total[left * NQ + 2 * h]
            b1 = total[left * NQ + 2 * h + 1]
            out[at, h] = jnp.where(
                low, a0 + jnp.roll(b0, 4, axis=0), jnp.roll(a1, 4, axis=0) + b1
            )
        return carry

    lax.fori_loop(0, NPLANE, body, 0)


def final_kernel(parts, given, out):
    low = low_half((8, 128))

    def body(h, carry):
        for half in range(2):
            base = given[2 * h + half].astype(jnp.float32)
            for i in range(16):
                a = parts[2 * i, h]
                b = parts[2 * i + 1, h]
                if half == 0:
                    tile = jnp.where(low, a, jnp.roll(b, 4, axis=0))
                else:
                    tile = jnp.where(low, jnp.roll(a, 4, axis=0), b)
                out[2 * h + half, 8 * i : 8 * i + 8, :] = base[8 * i : 8 * i + 8] - tile
        return carry

    lax.fori_loop(0, NQ // 2, body, 0)


def lists_of(rank, value, low, high):
    spots = jnp.arange(low, high, dtype=jnp.int32)
    return jnp.sum(
        jnp.where(rank[:, None, :] == spots[None, :, None], value[:, None, :], 0), axis=-1
    )


def on_device(block_ids, iface_counts, inv_factor, coupling, boundary_block):
    me = lax.axis_index("z")
    width = inv_factor.shape[1]
    tiles = []
    for member in range(2):
        rows = slice(member * width, (member + 1) * width)
        mixed = jnp.dot(
            inv_factor[rows], coupling[rows], preferred_element_type=jnp.float32
        ).astype(jnp.bfloat16)
        tiles.append(
            lax.dot_general(
                mixed,
                mixed[:, : CS * 128],
                (((0,), (0,)), ((), ())),
                preferred_element_type=jnp.float32,
            )
        )
    slices = pl.pallas_call(
        slice_kernel,
        out_shape=jax.ShapeDtypeStruct((NPLANE, SLOTS, 8, 128), jnp.float32),
        in_specs=[VMEM, VMEM],
        out_specs=VMEM,
    )(*tiles)
    spread = lax.all_to_all(slices, PLANE, 0, 0, tiled=True).reshape(NPLANE * SLOTS, 8, 128)

    slot = jnp.arange(8, dtype=jnp.int32)
    alive = (slot[None] >= CS) & (slot[None] < iface_counts[:, None])
    key = jnp.where(alive, block_ids, -1)
    key = key.reshape(YLO, NZ, NCOL * 16).transpose(1, 0, 2).reshape(NZ, NPLANE * 16)
    entry = jnp.arange(NPLANE * 16, dtype=jnp.int32)
    plane = jnp.where(key < 0, NZ, key & 15)
    own = lax.dynamic_index_in_dim(plane, me, 0, False)
    step = jnp.arange(NZ, dtype=jnp.int32)
    mask = jnp.concatenate([plane == me, own[None] == ((me + step) % NZ)[:, None]], axis=0)
    before = (entry[:, None] < entry[None, :]).astype(jnp.bfloat16)
    rank = jnp.dot(mask.astype(jnp.bfloat16), before, preferred_element_type=jnp.float32)
    rank = jnp.where(mask, rank.astype(jnp.int32), -1)
    spot = (((key >> 4) & 1) * NCOL + ((entry >> 4) & 15)[None]) * NQ + (key >> 5) - TRASH
    origin = (entry >> 4) * SLOTS + ((entry >> 3) & 1) * LIVE + (entry & 7) - CS
    value = jnp.concatenate([spot, jnp.broadcast_to(origin[None], (NZ, NPLANE * 16))], axis=0)
    table = lists_of(rank, value, 0, CAP)
    recv_list = (table[:NZ] + TRASH).reshape(-1)
    send_list = table[NZ:].reshape(-1)
    load = jnp.sum((plane[:, None, :] == step[None, :, None]).astype(jnp.int32), axis=-1)
    crowded = jnp.max(load) > CAP
    meta = me.astype(jnp.int32).reshape(1)

    packs = pl.pallas_call(
        pack_kernel,
        out_shape=[jax.ShapeDtypeStruct((CAP + CS, 8, 128), jnp.float32)] * NZ,
        in_specs=[SMEM, SMEM, VMEM],
        out_specs=[VMEM] * NZ,
    )(meta, send_list, spread)
    got = [packs[0]]
    for d in range(1, NZ):
        got.append(lax.ppermute(packs[d], "z", [(i, (i + d) % NZ) for i in range(NZ)]))
    total = pl.pallas_call(
        gather_kernel,
        out_shape=jax.ShapeDtypeStruct((TRASH + 1, 8, 128), jnp.float32),
        in_specs=[SMEM, SMEM] + [VMEM] * NZ,
        out_specs=VMEM,
    )(meta, recv_list, *got)

    def rest(total):
        more = lists_of(rank, value, CAP, FULL)
        mine = (more[:NZ] + TRASH).reshape(-1)
        theirs = more[NZ:]
        theirs = jnp.roll(theirs, me, axis=0).reshape(-1)
        buf = pl.pallas_call(
            rest_pack_kernel,
            out_shape=jax.ShapeDtypeStruct((NZ * (FULL - CAP), 8, 128), jnp.float32),
            in_specs=[SMEM, VMEM],
            out_specs=VMEM,
        )(theirs, spread)
        buf = lax.all_to_all(buf, "z", 0, 0, tiled=True)
        return pl.pallas_call(
            rest_gather_kernel,
            out_shape=jax.ShapeDtypeStruct((TRASH + 1, 8, 128), jnp.float32),
            in_specs=[SMEM, VMEM, VMEM],
            out_specs=VMEM,
        )(mine, buf, total)

    total = lax.cond(crowded, rest, lambda total: total, total)
    merged = pl.pallas_call(
        merge_kernel,
        out_shape=jax.ShapeDtypeStruct((NPLANE, NQ // 2, 8, 128), jnp.float32),
        in_specs=[VMEM],
        out_specs=VMEM,
    )(total)
    parts = lax.all_to_all(merged, PLANE, 0, 0, tiled=True)
    result = pl.pallas_call(
        final_kernel,
        out_shape=jax.ShapeDtypeStruct((NQ, 128, 128), jnp.float32),
        in_specs=[VMEM, VMEM],
        out_specs=VMEM,
    )(parts, boundary_block.reshape(NQ, 128, 128))
    return result.reshape(NQ, 128, 1, 128)


def solution(mesh):
    fine = Mesh(mesh.devices.reshape(YLO, NZ, XS, YHI, CORE), ("ylo", "z", "x", "yhi", "core"))
    row, col = ("ylo", "z"), ("x", "yhi", "core")
    return jax.shard_map(
        on_device,
        mesh=fine,
        in_specs=(
            P(),
            P(),
            P(row + col, None),
            P(row + col, None),
            P(None, row, None, col),
        ),
        out_specs=P(None, row, None, col),
        check_vma=False,
    )
```

time: 252 us -> 243 us (0.964)
  the two profiles are of different devices: /device:TPU:48 before, /device:TPU:1 now
where the time goes in v1:
time: 243 us; the launch traced here: 242 us
  starting transfers between devices  110 us (45%)
  waiting for transfers between devices  74.4 us (31%)
  blocking collectives  28.9 us (12%)
  Pallas kernels  16.3 us (7%)
  matrix products  6 us (2%)
  local copies, waits for them, and re-layouts  3.09 us (1%)
    ppermute x15, starting transfers between devices, on_device(): lax.ppermute(packs[d], 'z', [(i, (i + d) % NZ) for i in range(NZ)])  99.2 us
    ppermute x15, waiting for transfers between devices, on_device(): lax.ppermute(packs[d], 'z', [(i, (i + d) % NZ) for i in range(NZ)])  51.9 us
    all_to_all x1, blocking collectives, on_device(): parts = lax.all_to_all(merged, PLANE, 0, 0, tiled=True)  28.9 us
    all_to_all x1, waiting for transfers between devices, on_device(): lax.all_to_all(slices, PLANE, 0, 0, tiled=True)  22.5 us
    all_to_all x1, starting transfers between devices, on_device(): lax.all_to_all(slices, PLANE, 0, 0, tiled=True)  10.7 us
    pallas_call x1, Pallas kernels, on_device(): pl.pallas_call(gather_kernel, out_shape=jax.ShapeDtypeStruct((TRASH + 1,...  4.93 us
  transfers between devices with their start and end apart: 16, of which 8 were waited for; matrix products, arithmetic and copies ran while one was open for 2% of the time, Pallas kernels for 0%

profile of v1, /device:TPU:1, one launch (start us, length us, event | category | flops | bytes accessed | tf_op | source)
XLA Modules:
  0.0 241.8 jit_solution(7296783762090511822)
XLA Ops:
  0.0 2.2 convolution_convert_fusion
  2.9 1.5 fusion.5.second
  5.9 2.9 %shard_map.55 = f32[32,14,8,128]{3,2,1,0:T(8,128)} custom-call(f32[1024,256]{1,0:T(8,128)} %fusion.7.first, f32[1024,256]{1,0:T(8,128)} %fusion.5.second), custom_call_target="tpu_custom_call" | custom-call | tf_op jit(solution)/shard_map/pallas_call | solution.py:173
  8.8 10.7 %all-to-all-start.1 = ((f32[32,14,8,128]{3,2,1,0:T(8,128)}), f32[32,14,8,128]{3,2,1,0:T(8,128)S(1)}, u32[]{:S(2)}, u32[]{:S(2)}) async-start(f32[32,14,8,128]{3,2,1,0:T(8,128)} %shard_map.55), calls=%async_computation.1 | async-start | bytes 3670016 | tf_op jit(solution)/shard_map/all_to_all | solution.py:179
  23.0 22.5 %all-to-all-done.1 = f32[32,14,8,128]{3,2,1,0:T(8,128)S(1)} async-done(((f32[32,14,8,128]{3,2,1,0:T(8,128)}), f32[32,14,8,128]{3,2,1,0:T(8,128)S(1)}, u32[]{:S(2)}, u32[]{:S(2)}) %all-to-all-start.1) | async-done | bytes 1835040 | tf_op jit(solution)/shard_map/all_to_all | solution.py:179
  45.5 3.7 %shard_map.56 = (f32[38,8,128]{2,1,0:T(8,128)}, f32[38,8,128]{2,1,0:T(8,128)}, f32[38,8,128]{2,1,0:T(8,128)}, f32[38,8,128]{2,1,0:T(8,128)}, f32[38,8,128]{2,1,0...) custom-call(s32[1]{0:T(128)} %bitcast.1.meta, ...), custom_call_target="tpu_custom_call" | custom-call | tf_op jit(solution)/shard_map/pallas_call | solution.py:203
  49.2 1.9 collective-permute-start
  51.1 4.4 %collective-permute-start.1 = (f32[38,8,128]{2,1,0:T(8,128)}, f32[38,8,128]{2,1,0:T(8,128)S(1)}, u32[]{:S(2)}, u32[]{:S(2)}) collective-permute-start(f32[38,8,128]{2,1,0:T(8,128)} %get-tuple-element.42), channel_id=1, source_target_pairs={{0,32},{16,48},{32,64},{48,80},{64,96},{80,112},{96,128},{112,144}... | collective-permute-start | bytes 466952 | tf_op jit(solution)/shard_map/ppermute | solution.py:211
  55.5 7.5 %collective-permute-start.2 = (f32[38,8,128]{2,1,0:T(8,128)}, f32[38,8,128]{2,1,0:T(8,128)S(1)}, u32[]{:S(2)}, u32[]{:S(2)}) collective-permute-start(f32[38,8,128]{2,1,0:T(8,128)} %get-tuple-element.43), channel_id=1, source_target_pairs={{0,48},{16,64},{32,80},{48,96},{64,112},{80,128},{96,144},{112,160... | collective-permute-start | bytes 466952 | tf_op jit(solution)/shard_map/ppermute | solution.py:211
  63.0 7.0 %collective-permute-start.3 = (f32[38,8,128]{2,1,0:T(8,128)}, f32[38,8,128]{2,1,0:T(8,128)S(1)}, u32[]{:S(2)}, u32[]{:S(2)}) collective-permute-start(f32[38,8,128]{2,1,0:T(8,128)} %get-tuple-element.44), channel_id=1, source_target_pairs={{0,64},{16,80},{32,96},{48,112},{64,128},{80,144},{96,160},{112,17... | collective-permute-start | bytes 466952 | tf_op jit(solution)/shard_map/ppermute | solution.py:211
  70.0 4.5 %collective-permute-start.4 = (f32[38,8,128]{2,1,0:T(8,128)}, f32[38,8,128]{2,1,0:T(8,128)S(1)}, u32[]{:S(2)}, u32[]{:S(2)}) collective-permute-start(f32[38,8,128]{2,1,0:T(8,128)} %get-tuple-element.45), channel_id=1, source_target_pairs={{0,80},{16,96},{32,112},{48,128},{64,144},{80,160},{96,176},{112,1... | collective-permute-start | bytes 466952 | tf_op jit(solution)/shard_map/ppermute | solution.py:211
  74.5 3.4 %collective-permute-start.5 = (f32[38,8,128]{2,1,0:T(8,128)}, f32[38,8,128]{2,1,0:T(8,128)S(1)}, u32[]{:S(2)}, u32[]{:S(2)}) collective-permute-start(f32[38,8,128]{2,1,0:T(8,128)} %get-tuple-element.46), channel_id=1, source_target_pairs={{0,96},{16,112},{32,128},{48,144},{64,160},{80,176},{96,192},{112,... | collective-permute-start | bytes 466952 | tf_op jit(solution)/shard_map/ppermute | solution.py:211
  77.9 9.3 %collective-permute-start.6 = (f32[38,8,128]{2,1,0:T(8,128)}, f32[38,8,128]{2,1,0:T(8,128)S(1)}, u32[]{:S(2)}, u32[]{:S(2)}) collective-permute-start(f32[38,8,128]{2,1,0:T(8,128)} %get-tuple-element.47), channel_id=1, source_target_pairs={{0,112},{16,128},{32,144},{48,160},{64,176},{80,192},{96,208},{112... | collective-permute-start | bytes 466952 | tf_op jit(solution)/shard_map/ppermute | solution.py:211
  87.2 3.6 %collective-permute-start.7 = (f32[38,8,128]{2,1,0:T(8,128)}, f32[38,8,128]{2,1,0:T(8,128)S(1)}, u32[]{:S(2)}, u32[]{:S(2)}) collective-permute-start(f32[38,8,128]{2,1,0:T(8,128)} %get-tuple-element.48), channel_id=1, source_target_pairs={{0,128},{16,144},{32,160},{48,176},{64,192},{80,208},{96,224},{112... | collective-permute-start | bytes 466952 | tf_op jit(solution)/shard_map/ppermute | solution.py:211
  90.9 9.9 %collective-permute-start.8 = (f32[38,8,128]{2,1,0:T(8,128)}, f32[38,8,128]{2,1,0:T(8,128)}, u32[]{:S(2)}, u32[]{:S(2)}) collective-permute-start(f32[38,8,128]{2,1,0:T(8,128)} %get-tuple-element.49), channel_id=1, source_target_pairs={{0,144},{16,160},{32,176},{48,192},{64,208},{80,224},{96,240},{112... | collective-permute-start | bytes 466952 | tf_op jit(solution)/shard_map/ppermute | solution.py:211
  100.8 5.6 %collective-permute-done.4.refs_5_ = f32[38,8,128]{2,1,0:T(8,128)S(1)} collective-permute-done((f32[38,8,128]{2,1,0:T(8,128)}, f32[38,8,128]{2,1,0:T(8,128)S(1)}, u32[]{:S(2)}, u32[]{:S(2)}) %collective-permute-start.4) | collective-permute-done | bytes 155680 | tf_op jit(solution)/shard_map/ppermute | solution.py:211
  106.4 8.3 %collective-permute-start.9 = (f32[38,8,128]{2,1,0:T(8,128)}, f32[38,8,128]{2,1,0:T(8,128)}, u32[]{:S(2)}, u32[]{:S(2)}) collective-permute-start(f32[38,8,128]{2,1,0:T(8,128)} %get-tuple-element.50), channel_id=1, source_target_pairs={{0,160},{16,176},{32,192},{48,208},{64,224},{80,240},{96,0},{112,1... | collective-permute-start | bytes 466952 | tf_op jit(solution)/shard_map/ppermute | solution.py:211
  116.5 5.1 %collective-permute-done.5.refs_6_ = f32[38,8,128]{2,1,0:T(8,128)S(1)} collective-permute-done((f32[38,8,128]{2,1,0:T(8,128)}, f32[38,8,128]{2,1,0:T(8,128)S(1)}, u32[]{:S(2)}, u32[]{:S(2)}) %collective-permute-start.5) | collective-permute-done | bytes 155680 | tf_op jit(solution)/shard_map/ppermute | solution.py:211
  121.6 19.1 %collective-permute-start.10 = (f32[38,8,128]{2,1,0:T(8,128)}, f32[38,8,128]{2,1,0:T(8,128)}, u32[]{:S(2)}, u32[]{:S(2)}) collective-permute-start(f32[38,8,128]{2,1,0:T(8,128)} %get-tuple-element.51), channel_id=1, source_target_pairs={{0,176},{16,192},{32,208},{48,224},{64,240},{80,0},{96,16},{112,32... | collective-permute-start | bytes 466952 | tf_op jit(solution)/shard_map/ppermute | solution.py:211
  140.6 17.5 %collective-permute-done.6.refs_7_ = f32[38,8,128]{2,1,0:T(8,128)S(1)} collective-permute-done((f32[38,8,128]{2,1,0:T(8,128)}, f32[38,8,128]{2,1,0:T(8,128)S(1)}, u32[]{:S(2)}, u32[]{:S(2)}) %collective-permute-start.6) | collective-permute-done | bytes 155680 | tf_op jit(solution)/shard_map/ppermute | solution.py:211
  158.1 13.9 %collective-permute-start.11 = (f32[38,8,128]{2,1,0:T(8,128)}, f32[38,8,128]{2,1,0:T(8,128)}, u32[]{:S(2)}, u32[]{:S(2)}) collective-permute-start(f32[38,8,128]{2,1,0:T(8,128)} %get-tuple-element.52), channel_id=1, source_target_pairs={{0,192},{16,208},{32,224},{48,240},{64,0},{80,16},{96,32},{112,48}... | collective-permute-start | bytes 466952 | tf_op jit(solution)/shard_map/ppermute | solution.py:211
  172.0 1.9 collective-permute-start.12
  173.9 2.7 %collective-permute-start.13 = (f32[38,8,128]{2,1,0:T(8,128)}, f32[38,8,128]{2,1,0:T(8,128)}, u32[]{:S(2)}, u32[]{:S(2)}) collective-permute-start(f32[38,8,128]{2,1,0:T(8,128)} %get-tuple-element.54), channel_id=1, source_target_pairs={{0,224},{16,240},{32,0},{48,16},{64,32},{80,48},{96,64},{112,80},{... | collective-permute-start | bytes 466952 | tf_op jit(solution)/shard_map/ppermute | solution.py:211
  176.7 1.9 collective-permute-start.14
  179.3 3.3 %collective-permute-done.11.refs_12_ = f32[38,8,128]{2,1,0:T(8,128)} collective-permute-done((f32[38,8,128]{2,1,0:T(8,128)}, f32[38,8,128]{2,1,0:T(8,128)}, u32[]{:S(2)}, u32[]{:S(2)}) %collective-permute-start.11) | collective-permute-done | bytes 155680 | tf_op jit(solution)/shard_map/ppermute | solution.py:211
  182.6 13.9 %collective-permute-done.12.refs_13_ = f32[38,8,128]{2,1,0:T(8,128)} collective-permute-done((f32[38,8,128]{2,1,0:T(8,128)}, f32[38,8,128]{2,1,0:T(8,128)}, u32[]{:S(2)}, u32[]{:S(2)}) %collective-permute-start.12) | collective-permute-done | bytes 155680 | tf_op jit(solution)/shard_map/ppermute | solution.py:211
  196.5 1.5 collective-permute-done.13.refs_14_
  198.0 5.0 %collective-permute-done.14.refs_15_ = f32[38,8,128]{2,1,0:T(8,128)} collective-permute-done((f32[38,8,128]{2,1,0:T(8,128)}, f32[38,8,128]{2,1,0:T(8,128)}, u32[]{:S(2)}, u32[]{:S(2)}) %collective-permute-start.14) | collective-permute-done | bytes 155680 | tf_op jit(solution)/shard_map/ppermute | solution.py:211
  203.1 4.9 %shard_map.57 = f32[769,8,128]{2,1,0:T(8,128)S(1)} custom-call(s32[1]{0:T(128)} %bitcast.1.meta, s32[576]{0:T(1024)} %reshape.110.recv_list, f32[38,8,128]{2,1,0:T(8,128)} %get-tuple-element.40.refs_0_, f32[38,8,128]{2,1,0:T(8,128)} %copy-done.1, f32[38,8,128]{2,1,0:T(8,128)} %copy-done.2, f32[38,8,128]{2,1,0:T(8,128)} %copy-done.3, ...), custom_call_target="tpu_custom_call" | custom-call | tf_op jit(solution)/shard_map/pallas_call | solution.py:212
  208.0 1.7 shard_map.58
  209.8 28.9 %all_to_all.14.parts = f32[32,12,8,128]{3,2,1,0:T(8,128)} all-to-all(f32[32,12,8,128]{3,2,1,0:T(8,128)} %shard_map.58), channel_id=1, replica_groups=mesh['ylo'=2,'z'=16,'x'=4,'yhi'=2,'core'=2] {'ylo','x','yhi','core'}, dimensions={0} | all-to-all | bytes 3145728 | tf_op jit(solution)/shard_map/all_to_all | solution.py:245
  238.7 3.1 %shard_map.59 = f32[24,128,128]{2,1,0:T(8,128)} custom-call(f32[32,12,8,128]{3,2,1,0:T(8,128)} %all_to_all.14.parts, bf16[24,128,128]{2,1,0:T(8,128)(2,1)} %bitcast.20), custom_call_target="tpu_custom_call" | custom-call | tf_op jit(solution)/shard_map/pallas_call | solution.py:246
  (66 shorter events, 7.4 us)
Async XLA Ops:
  0.0 2.2 copy-start.11
  0.0 2.2 copy-start.12
  8.8 10.7 %copy-start.9 = (s32[1024,8]{0,1:T(8,128)S(1)}, s32[1024,8]{0,1:T(8,128)}, u32[]{:S(2)}) copy-start(s32[1024,8]{0,1:T(8,128)} %param.7) | copy-start | bytes 98308
  8.8 10.7 %copy-start.10 = (s32[1024]{0:T(1024)S(1)}, s32[1024]{0:T(1024)}, u32[]{:S(2)}) copy-start(s32[1024]{0:T(1024)} %param.8) | copy-start | bytes 12292
  8.8 36.7 %all-to-all-start.1 = ((f32[32,14,8,128]{3,2,1,0:T(8,128)}), f32[32,14,8,128]{3,2,1,0:T(8,128)S(1)}, u32[]{:S(2)}, u32[]{:S(2)}) async-start(f32[32,14,8,128]{3,2,1,0:T(8,128)} %shard_map.55), calls=%async_computation.1 | async-start | bytes 3670016 | tf_op jit(solution)/shard_map/all_to_all | solution.py:179
  45.5 157.5 %copy-start = (f32[32,14,8,128]{3,2,1,0:T(8,128)}, f32[32,14,8,128]{3,2,1,0:T(8,128)S(1)}, u32[]{:S(2)}) copy-start(f32[32,14,8,128]{3,2,1,0:T(8,128)S(1)} %all-to-all-done.1) | copy-start | bytes 5505028
  49.2 25.3 %collective-permute-start = (f32[38,8,128]{2,1,0:T(8,128)}, f32[38,8,128]{2,1,0:T(8,128)S(1)}, u32[]{:S(2)}, u32[]{:S(2)}) collective-permute-start(f32[38,8,128]{2,1,0:T(8,128)} %get-tuple-element.41), channel_id=1, source_target_pairs={{0,16},{16,32},{32,48},{48,64},{64,80},{80,96},{96,112},{112,128},... | collective-permute-start | bytes 466952 | tf_op jit(solution)/shard_map/ppermute | solution.py:211
  51.1 26.8 %collective-permute-start.1 = (f32[38,8,128]{2,1,0:T(8,128)}, f32[38,8,128]{2,1,0:T(8,128)S(1)}, u32[]{:S(2)}, u32[]{:S(2)}) collective-permute-start(f32[38,8,128]{2,1,0:T(8,128)} %get-tuple-element.42), channel_id=1, source_target_pairs={{0,32},{16,48},{32,64},{48,80},{64,96},{80,112},{96,128},{112,144}... | collective-permute-start | bytes 466952 | tf_op jit(solution)/shard_map/ppermute | solution.py:211
  55.5 31.7 %collective-permute-start.2 = (f32[38,8,128]{2,1,0:T(8,128)}, f32[38,8,128]{2,1,0:T(8,128)S(1)}, u32[]{:S(2)}, u32[]{:S(2)}) collective-permute-start(f32[38,8,128]{2,1,0:T(8,128)} %get-tuple-element.43), channel_id=1, source_target_pairs={{0,48},{16,64},{32,80},{48,96},{64,112},{80,128},{96,144},{112,160... | collective-permute-start | bytes 466952 | tf_op jit(solution)/shard_map/ppermute | solution.py:211
  63.0 27.8 %collective-permute-start.3 = (f32[38,8,128]{2,1,0:T(8,128)}, f32[38,8,128]{2,1,0:T(8,128)S(1)}, u32[]{:S(2)}, u32[]{:S(2)}) collective-permute-start(f32[38,8,128]{2,1,0:T(8,128)} %get-tuple-element.44), channel_id=1, source_target_pairs={{0,64},{16,80},{32,96},{48,112},{64,128},{80,144},{96,160},{112,17... | collective-permute-start | bytes 466952 | tf_op jit(solution)/shard_map/ppermute | solution.py:211
  70.0 36.4 %collective-permute-start.4 = (f32[38,8,128]{2,1,0:T(8,128)}, f32[38,8,128]{2,1,0:T(8,128)S(1)}, u32[]{:S(2)}, u32[]{:S(2)}) collective-permute-start(f32[38,8,128]{2,1,0:T(8,128)} %get-tuple-element.45), channel_id=1, source_target_pairs={{0,80},{16,96},{32,112},{48,128},{64,144},{80,160},{96,176},{112,1... | collective-permute-start | bytes 466952 | tf_op jit(solution)/shard_map/ppermute | solution.py:211
  74.5 128.6 %copy-start.1 = (f32[38,8,128]{2,1,0:T(8,128)}, f32[38,8,128]{2,1,0:T(8,128)S(1)}, u32[]{:S(2)}) copy-start(f32[38,8,128]{2,1,0:T(8,128)S(1)} %collective-permute-done.refs_1_) | copy-start | bytes 466948
  74.5 47.0 %collective-permute-start.5 = (f32[38,8,128]{2,1,0:T(8,128)}, f32[38,8,128]{2,1,0:T(8,128)S(1)}, u32[]{:S(2)}, u32[]{:S(2)}) collective-permute-start(f32[38,8,128]{2,1,0:T(8,128)} %get-tuple-element.46), channel_id=1, source_target_pairs={{0,96},{16,112},{32,128},{48,144},{64,160},{80,176},{96,192},{112,... | collective-permute-start | bytes 466952 | tf_op jit(solution)/shard_map/ppermute | solution.py:211
  77.9 125.1 %copy-start.2 = (f32[38,8,128]{2,1,0:T(8,128)}, f32[38,8,128]{2,1,0:T(8,128)S(1)}, u32[]{:S(2)}) copy-start(f32[38,8,128]{2,1,0:T(8,128)S(1)} %collective-permute-done.1.refs_2_) | copy-start | bytes 466948
  77.9 80.2 %collective-permute-start.6 = (f32[38,8,128]{2,1,0:T(8,128)}, f32[38,8,128]{2,1,0:T(8,128)S(1)}, u32[]{:S(2)}, u32[]{:S(2)}) collective-permute-start(f32[38,8,128]{2,1,0:T(8,128)} %get-tuple-element.47), channel_id=1, source_target_pairs={{0,112},{16,128},{32,144},{48,160},{64,176},{80,192},{96,208},{112... | collective-permute-start | bytes 466952 | tf_op jit(solution)/shard_map/ppermute | solution.py:211
  87.2 115.8 %copy-start.3 = (f32[38,8,128]{2,1,0:T(8,128)}, f32[38,8,128]{2,1,0:T(8,128)S(1)}, u32[]{:S(2)}) copy-start(f32[38,8,128]{2,1,0:T(8,128)S(1)} %collective-permute-done.2.refs_3_) | copy-start | bytes 466948
  87.2 84.8 %collective-permute-start.7 = (f32[38,8,128]{2,1,0:T(8,128)}, f32[38,8,128]{2,1,0:T(8,128)S(1)}, u32[]{:S(2)}, u32[]{:S(2)}) collective-permute-start(f32[38,8,128]{2,1,0:T(8,128)} %get-tuple-element.48), channel_id=1, source_target_pairs={{0,128},{16,144},{32,160},{48,176},{64,192},{80,208},{96,224},{112... | collective-permute-start | bytes 466952 | tf_op jit(solution)/shard_map/ppermute | solution.py:211
  90.8 112.2 %copy-start.4 = (f32[38,8,128]{2,1,0:T(8,128)}, f32[38,8,128]{2,1,0:T(8,128)S(1)}, u32[]{:S(2)}) copy-start(f32[38,8,128]{2,1,0:T(8,128)S(1)} %collective-permute-done.3.refs_4_) | copy-start | bytes 466948
  90.9 83.1 %collective-permute-start.8 = (f32[38,8,128]{2,1,0:T(8,128)}, f32[38,8,128]{2,1,0:T(8,128)}, u32[]{:S(2)}, u32[]{:S(2)}) collective-permute-start(f32[38,8,128]{2,1,0:T(8,128)} %get-tuple-element.49), channel_id=1, source_target_pairs={{0,144},{16,160},{32,176},{48,192},{64,208},{80,224},{96,240},{112... | collective-permute-start | bytes 466952 | tf_op jit(solution)/shard_map/ppermute | solution.py:211
  106.4 96.7 %copy-start.5 = (f32[38,8,128]{2,1,0:T(8,128)}, f32[38,8,128]{2,1,0:T(8,128)S(1)}, u32[]{:S(2)}) copy-start(f32[38,8,128]{2,1,0:T(8,128)S(1)} %collective-permute-done.4.refs_5_) | copy-start | bytes 466948
  106.4 70.3 %collective-permute-start.9 = (f32[38,8,128]{2,1,0:T(8,128)}, f32[38,8,128]{2,1,0:T(8,128)}, u32[]{:S(2)}, u32[]{:S(2)}) collective-permute-start(f32[38,8,128]{2,1,0:T(8,128)} %get-tuple-element.50), channel_id=1, source_target_pairs={{0,160},{16,176},{32,192},{48,208},{64,224},{80,240},{96,0},{112,1... | collective-permute-start | bytes 466952 | tf_op jit(solution)/shard_map/ppermute | solution.py:211
  121.5 81.5 %copy-start.6 = (f32[38,8,128]{2,1,0:T(8,128)}, f32[38,8,128]{2,1,0:T(8,128)S(1)}, u32[]{:S(2)}) copy-start(f32[38,8,128]{2,1,0:T(8,128)S(1)} %collective-permute-done.5.refs_6_) | copy-start | bytes 466948
  121.6 57.7 %collective-permute-start.10 = (f32[38,8,128]{2,1,0:T(8,128)}, f32[38,8,128]{2,1,0:T(8,128)}, u32[]{:S(2)}, u32[]{:S(2)}) collective-permute-start(f32[38,8,128]{2,1,0:T(8,128)} %get-tuple-element.51), channel_id=1, source_target_pairs={{0,176},{16,192},{32,208},{48,224},{64,240},{80,0},{96,16},{112,32... | collective-permute-start | bytes 466952 | tf_op jit(solution)/shard_map/ppermute | solution.py:211
  158.1 45.0 %copy-start.7 = (f32[38,8,128]{2,1,0:T(8,128)}, f32[38,8,128]{2,1,0:T(8,128)S(1)}, u32[]{:S(2)}) copy-start(f32[38,8,128]{2,1,0:T(8,128)S(1)} %collective-permute-done.6.refs_7_) | copy-start | bytes 466948
  158.1 24.5 %collective-permute-start.11 = (f32[38,8,128]{2,1,0:T(8,128)}, f32[38,8,128]{2,1,0:T(8,128)}, u32[]{:S(2)}, u32[]{:S(2)}) collective-permute-start(f32[38,8,128]{2,1,0:T(8,128)} %get-tuple-element.52), channel_id=1, source_target_pairs={{0,192},{16,208},{32,224},{48,240},{64,0},{80,16},{96,32},{112,48}... | collective-permute-start | bytes 466952 | tf_op jit(solution)/shard_map/ppermute | solution.py:211
  172.0 31.1 %copy-start.8 = (f32[38,8,128]{2,1,0:T(8,128)}, f32[38,8,128]{2,1,0:T(8,128)S(1)}, u32[]{:S(2)}) copy-start(f32[38,8,128]{2,1,0:T(8,128)S(1)} %collective-permute-done.7.refs_8_) | copy-start | bytes 466948
  172.0 24.5 %collective-permute-start.12 = (f32[38,8,128]{2,1,0:T(8,128)}, f32[38,8,128]{2,1,0:T(8,128)}, u32[]{:S(2)}, u32[]{:S(2)}) collective-permute-start(f32[38,8,128]{2,1,0:T(8,128)} %get-tuple-element.53), channel_id=1, source_target_pairs={{0,208},{16,224},{32,240},{48,0},{64,16},{80,32},{96,48},{112,64},... | collective-permute-start | bytes 466952 | tf_op jit(solution)/shard_map/ppermute | solution.py:211
  173.9 24.1 %collective-permute-start.13 = (f32[38,8,128]{2,1,0:T(8,128)}, f32[38,8,128]{2,1,0:T(8,128)}, u32[]{:S(2)}, u32[]{:S(2)}) collective-permute-start(f32[38,8,128]{2,1,0:T(8,128)} %get-tuple-element.54), channel_id=1, source_target_pairs={{0,224},{16,240},{32,0},{48,16},{64,32},{80,48},{96,64},{112,80},{... | collective-permute-start | bytes 466952 | tf_op jit(solution)/shard_map/ppermute | solution.py:211
  176.7 26.3 %collective-permute-start.14 = (f32[38,8,128]{2,1,0:T(8,128)}, f32[38,8,128]{2,1,0:T(8,128)}, u32[]{:S(2)}, u32[]{:S(2)}) collective-permute-start(f32[38,8,128]{2,1,0:T(8,128)} %get-tuple-element.55), channel_id=1, source_target_pairs={{0,240},{16,0},{32,16},{48,32},{64,48},{80,64},{96,80},{112,96},{1... | collective-permute-start | bytes 466952 | tf_op jit(solution)/shard_map/ppermute | solution.py:211

commit v2 on v1

--- a/solution.py
+++ b/solution.py
@@ -15,8 +15,9 @@
 LIVE = 6
 SLOTS = 2 * LIVE + CS
 NQ = 24
-CAP = 36
+CAP = 34
 FULL = 64
+OFFSETS = (0, 8, 7, 9, 6, 10, 5, 11, 4, 12, 3, 13, 2, 14, 1, 15)
 TRASH = NPLANE * NQ
 VMEM = pl.BlockSpec(memory_space=pltpu.VMEM)
 SMEM = pl.BlockSpec(memory_space=pltpu.SMEM)
@@ -53,8 +54,8 @@
 
 def pack_kernel(meta, send_list, slices, *outs):
     me = meta[0]
-    for d in range(NZ):
-        out = outs[d]
+    for at, d in enumerate(OFFSETS):
+        out = outs[at]
 
         def body(p, carry, d=d, out=out):
             out[p] = slices[send_list[d * CAP + p]]
@@ -74,8 +75,8 @@
     bufs, total = refs[:NZ], refs[NZ]
     me = meta[0]
     total[...] = jnp.zeros_like(total)
-    for d in range(NZ):
-        buf = bufs[d]
+    for at, d in enumerate(OFFSETS):
+        buf = bufs[at]
         base = lax.rem(me + NZ - d, NZ) * CAP
         for k in range(CS):
             spot = lax.rem(me + NZ - k, NZ) * NQ
@@ -207,8 +208,8 @@
         out_specs=[VMEM] * NZ,
     )(meta, send_list, spread)
     got = [packs[0]]
-    for d in range(1, NZ):
-        got.append(lax.ppermute(packs[d], "z", [(i, (i + d) % NZ) for i in range(NZ)]))
+    for at, d in list(enumerate(OFFSETS))[1:]:
+        got.append(lax.ppermute(packs[at], "z", [(i, (i + d) % NZ) for i in range(NZ)]))
     total = pl.pallas_call(
         gather_kernel,
         out_shape=jax.ShapeDtypeStruct((TRASH + 1, 8, 128), jnp.float32),

time: 243 us -> 204 us (0.84)
  waiting for transfers between devices: 74.4 us -> 54.7 us
  starting transfers between devices: 110 us -> 93.1 us
    ppermute x15, waiting for transfers between devices: 51.9 us -> 32.1 us  [on_device(): lax.ppermute(packs[at], 'z', [(i, (i + d) % NZ) for i in range(NZ)])]
    ppermute x15, starting transfers between devices: 99.2 us -> 82.5 us  [on_device(): lax.ppermute(packs[at], 'z', [(i, (i + d) % NZ) for i in range(NZ)])]
  transfers between devices with their start and end apart: 16 -> 16, of which waited for: 8 -> 6; matrix products, arithmetic and copies ran while one was open for 2% -> 2% of each run, Pallas kernels for 0% -> 0%
where the time goes in v2:
time: 204 us
  starting transfers between devices  93.1 us (46%)
  waiting for transfers between devices  54.7 us (27%)
  blocking collectives  27.8 us (14%)
  Pallas kernels  15.9 us (8%)
  matrix products  5.98 us (3%)
  local copies, waits for them, and re-layouts  3.11 us (2%)
    ppermute x15, starting transfers between devices, on_device(): lax.ppermute(packs[at], 'z', [(i, (i + d) % NZ) for i in range(NZ)])  82.5 us
    ppermute x15, waiting for transfers between devices, on_device(): lax.ppermute(packs[at], 'z', [(i, (i + d) % NZ) for i in range(NZ)])  32.1 us
    all_to_all x1, blocking collectives, on_device(): parts = lax.all_to_all(merged, PLANE, 0, 0, tiled=True)  27.8 us
    all_to_all x1, waiting for transfers between devices, on_device(): lax.all_to_all(slices, PLANE, 0, 0, tiled=True)  22.6 us
    all_to_all x1, starting transfers between devices, on_device(): lax.all_to_all(slices, PLANE, 0, 0, tiled=True)  10.7 us
    pallas_call x1, Pallas kernels, on_device(): pl.pallas_call(gather_kernel, out_shape=jax.ShapeDtypeStruct((TRASH + 1,...  4.47 us
  transfers between devices with their start and end apart: 16, of which 6 were waited for; matrix products, arithmetic and copies ran while one was open for 2% of the time, Pallas kernels for 0%

profile of v2, /device:TPU:1, one launch (start us, length us, event | category | flops | bytes accessed | tf_op | source)
XLA Modules:
  0.0 203.5 jit_solution(15274258553396361390)
XLA Ops:
  0.0 2.2 %convolution_convert_fusion = bf16[472,1024]{1,0:T(8,128)(2,1)S(1)} fusion(bf16[944,1024]{1,0:T(8,128)(2,1)} %param.10, bf16[944,472]{1,0:T(8,128)(2,1)} %param.9), kind=kOutput, calls=%fused_computation.6 | convolution fusion | flops 456744960 | bytes 2416640 | tf_op jit(solution)/shard_map/dot_general | solution.py:163
  2.9 1.5 fusion.5.second
  4.4 1.5 fusion.7.first
  5.8 2.9 %shard_map.55 = f32[32,14,8,128]{3,2,1,0:T(8,128)} custom-call(f32[1024,256]{1,0:T(8,128)} %fusion.7.first, f32[1024,256]{1,0:T(8,128)} %fusion.5.second), custom_call_target="tpu_custom_call" | custom-call | tf_op jit(solution)/shard_map/pallas_call | solution.py:174
  8.8 10.7 %all-to-all-start.1 = ((f32[32,14,8,128]{3,2,1,0:T(8,128)}), f32[32,14,8,128]{3,2,1,0:T(8,128)S(1)}, u32[]{:S(2)}, u32[]{:S(2)}) async-start(f32[32,14,8,128]{3,2,1,0:T(8,128)} %shard_map.55), calls=%async_computation.1 | async-start | bytes 3670016 | tf_op jit(solution)/shard_map/all_to_all | solution.py:180
  22.2 0.7 reshape.111.send_list
  22.9 22.6 %all-to-all-done.1 = f32[32,14,8,128]{3,2,1,0:T(8,128)S(1)} async-done(((f32[32,14,8,128]{3,2,1,0:T(8,128)}), f32[32,14,8,128]{3,2,1,0:T(8,128)S(1)}, u32[]{:S(2)}, u32[]{:S(2)}) %all-to-all-start.1) | async-done | bytes 1835040 | tf_op jit(solution)/shard_map/all_to_all | solution.py:180
  45.5 3.7 %shard_map.56 = (f32[36,8,128]{2,1,0:T(8,128)}, f32[36,8,128]{2,1,0:T(8,128)}, f32[36,8,128]{2,1,0:T(8,128)}, f32[36,8,128]{2,1,0:T(8,128)}, f32[36,8,128]{2,1,0...) custom-call(s32[1]{0:T(128)} %bitcast.1.meta, ...), custom_call_target="tpu_custom_call" | custom-call | tf_op jit(solution)/shard_map/pallas_call | solution.py:204
  49.1 13.3 %collective-permute-start = (f32[36,8,128]{2,1,0:T(8,128)}, f32[36,8,128]{2,1,0:T(8,128)S(1)}, u32[]{:S(2)}, u32[]{:S(2)}) collective-permute-start(f32[36,8,128]{2,1,0:T(8,128)} %get-tuple-element.41), channel_id=1, source_target_pairs={{0,128},{16,144},{32,160},{48,176},{64,192},{80,208},{96,224},{112... | collective-permute-start | bytes 442376 | tf_op jit(solution)/shard_map/ppermute | solution.py:212
  62.5 5.4 %collective-permute-start.1 = (f32[36,8,128]{2,1,0:T(8,128)}, f32[36,8,128]{2,1,0:T(8,128)S(1)}, u32[]{:S(2)}, u32[]{:S(2)}) collective-permute-start(f32[36,8,128]{2,1,0:T(8,128)} %get-tuple-element.42), channel_id=1, source_target_pairs={{0,112},{16,128},{32,144},{48,160},{64,176},{80,192},{96,208},{112... | collective-permute-start | bytes 442376 | tf_op jit(solution)/shard_map/ppermute | solution.py:212
  67.9 7.7 %collective-permute-start.2 = (f32[36,8,128]{2,1,0:T(8,128)}, f32[36,8,128]{2,1,0:T(8,128)S(1)}, u32[]{:S(2)}, u32[]{:S(2)}) collective-permute-start(f32[36,8,128]{2,1,0:T(8,128)} %get-tuple-element.43), channel_id=1, source_target_pairs={{0,144},{16,160},{32,176},{48,192},{64,208},{80,224},{96,240},{112... | collective-permute-start | bytes 442376 | tf_op jit(solution)/shard_map/ppermute | solution.py:212
  75.6 4.9 %collective-permute-start.3 = (f32[36,8,128]{2,1,0:T(8,128)}, f32[36,8,128]{2,1,0:T(8,128)S(1)}, u32[]{:S(2)}, u32[]{:S(2)}) collective-permute-start(f32[36,8,128]{2,1,0:T(8,128)} %get-tuple-element.44), channel_id=1, source_target_pairs={{0,96},{16,112},{32,128},{48,144},{64,160},{80,176},{96,192},{112,... | collective-permute-start | bytes 442376 | tf_op jit(solution)/shard_map/ppermute | solution.py:212
  80.5 7.3 %collective-permute-start.4 = (f32[36,8,128]{2,1,0:T(8,128)}, f32[36,8,128]{2,1,0:T(8,128)S(1)}, u32[]{:S(2)}, u32[]{:S(2)}) collective-permute-start(f32[36,8,128]{2,1,0:T(8,128)} %get-tuple-element.45), channel_id=1, source_target_pairs={{0,160},{16,176},{32,192},{48,208},{64,224},{80,240},{96,0},{112,1... | collective-permute-start | bytes 442376 | tf_op jit(solution)/shard_map/ppermute | solution.py:212
  87.8 4.5 %collective-permute-start.5 = (f32[36,8,128]{2,1,0:T(8,128)}, f32[36,8,128]{2,1,0:T(8,128)S(1)}, u32[]{:S(2)}, u32[]{:S(2)}) collective-permute-start(f32[36,8,128]{2,1,0:T(8,128)} %get-tuple-element.46), channel_id=1, source_target_pairs={{0,80},{16,96},{32,112},{48,128},{64,144},{80,160},{96,176},{112,1... | collective-permute-start | bytes 442376 | tf_op jit(solution)/shard_map/ppermute | solution.py:212
  92.3 16.2 %collective-permute-done.1.refs_2_ = f32[36,8,128]{2,1,0:T(8,128)S(1)} collective-permute-done((f32[36,8,128]{2,1,0:T(8,128)}, f32[36,8,128]{2,1,0:T(8,128)S(1)}, u32[]{:S(2)}, u32[]{:S(2)}) %collective-permute-start.1) | collective-permute-done | bytes 147488 | tf_op jit(solution)/shard_map/ppermute | solution.py:212
  108.5 1.9 collective-permute-start.6
  110.5 1.9 collective-permute-start.7
  112.4 7.3 %collective-permute-start.8 = (f32[36,8,128]{2,1,0:T(8,128)}, f32[36,8,128]{2,1,0:T(8,128)S(1)}, u32[]{:S(2)}, u32[]{:S(2)}) collective-permute-start(f32[36,8,128]{2,1,0:T(8,128)} %get-tuple-element.49), channel_id=1, source_target_pairs={{0,192},{16,208},{32,224},{48,240},{64,0},{80,16},{96,32},{112,48}... | collective-permute-start | bytes 442376 | tf_op jit(solution)/shard_map/ppermute | solution.py:212
  119.7 6.5 %collective-permute-start.9 = (f32[36,8,128]{2,1,0:T(8,128)}, f32[36,8,128]{2,1,0:T(8,128)}, u32[]{:S(2)}, u32[]{:S(2)}) collective-permute-start(f32[36,8,128]{2,1,0:T(8,128)} %get-tuple-element.50), channel_id=1, source_target_pairs={{0,48},{16,64},{32,80},{48,96},{64,112},{80,128},{96,144},{112,160... | collective-permute-start | bytes 442376 | tf_op jit(solution)/shard_map/ppermute | solution.py:212
  127.8 9.8 %collective-permute-done.5.refs_6_ = f32[36,8,128]{2,1,0:T(8,128)S(1)} collective-permute-done((f32[36,8,128]{2,1,0:T(8,128)}, f32[36,8,128]{2,1,0:T(8,128)S(1)}, u32[]{:S(2)}, u32[]{:S(2)}) %collective-permute-start.5) | collective-permute-done | bytes 147488 | tf_op jit(solution)/shard_map/ppermute | solution.py:212
  137.6 1.9 collective-permute-start.10
  139.6 1.9 collective-permute-start.11
  141.5 5.5 %collective-permute-start.12 = (f32[36,8,128]{2,1,0:T(8,128)}, f32[36,8,128]{2,1,0:T(8,128)}, u32[]{:S(2)}, u32[]{:S(2)}) collective-permute-start(f32[36,8,128]{2,1,0:T(8,128)} %get-tuple-element.53), channel_id=1, source_target_pairs={{0,224},{16,240},{32,0},{48,16},{64,32},{80,48},{96,64},{112,80},{... | collective-permute-start | bytes 442376 | tf_op jit(solution)/shard_map/ppermute | solution.py:212
  147.0 7.7 %collective-permute-start.13 = (f32[36,8,128]{2,1,0:T(8,128)}, f32[36,8,128]{2,1,0:T(8,128)}, u32[]{:S(2)}, u32[]{:S(2)}) collective-permute-start(f32[36,8,128]{2,1,0:T(8,128)} %get-tuple-element.54), channel_id=1, source_target_pairs={{0,16},{16,32},{32,48},{48,64},{64,80},{80,96},{96,112},{112,128},... | collective-permute-start | bytes 442376 | tf_op jit(solution)/shard_map/ppermute | solution.py:212
  154.8 4.8 %collective-permute-start.14 = (f32[36,8,128]{2,1,0:T(8,128)}, f32[36,8,128]{2,1,0:T(8,128)}, u32[]{:S(2)}, u32[]{:S(2)}) collective-permute-start(f32[36,8,128]{2,1,0:T(8,128)} %get-tuple-element.55), channel_id=1, source_target_pairs={{0,240},{16,0},{32,16},{48,32},{64,48},{80,64},{96,80},{112,96},{1... | collective-permute-start | bytes 442376 | tf_op jit(solution)/shard_map/ppermute | solution.py:212
  160.3 1.8 collective-permute-done.12.refs_13_
  162.0 1.7 collective-permute-done.13.refs_14_
  163.7 2.6 %collective-permute-done.14.refs_15_ = f32[36,8,128]{2,1,0:T(8,128)} collective-permute-done((f32[36,8,128]{2,1,0:T(8,128)}, f32[36,8,128]{2,1,0:T(8,128)}, u32[]{:S(2)}, u32[]{:S(2)}) %collective-permute-start.14) | collective-permute-done | bytes 147488 | tf_op jit(solution)/shard_map/ppermute | solution.py:212
  166.4 4.5 %shard_map.57 = f32[769,8,128]{2,1,0:T(8,128)S(1)} custom-call(s32[1]{0:T(128)} %bitcast.1.meta, s32[544]{0:T(1024)} %reshape.110.recv_list, f32[36,8,128]{2,1,0:T(8,128)} %get-tuple-element.40.refs_0_, f32[36,8,128]{2,1,0:T(8,128)} %copy-done.1, f32[36,8,128]{2,1,0:T(8,128)} %copy-done.2, f32[36,8,128]{2,1,0:T(8,128)} %copy-done.3, ...), custom_call_target="tpu_custom_call" | custom-call | tf_op jit(solution)/shard_map/pallas_call | solution.py:213
  170.9 1.7 shard_map.58
  172.6 27.8 %all_to_all.14.parts = f32[32,12,8,128]{3,2,1,0:T(8,128)} all-to-all(f32[32,12,8,128]{3,2,1,0:T(8,128)} %shard_map.58), channel_id=1, replica_groups=mesh['ylo'=2,'z'=16,'x'=4,'yhi'=2,'core'=2] {'ylo','x','yhi','core'}, dimensions={0} | all-to-all | bytes 3145728 | tf_op jit(solution)/shard_map/all_to_all | solution.py:246
  200.4 3.1 %shard_map.59 = f32[24,128,128]{2,1,0:T(8,128)} custom-call(f32[32,12,8,128]{3,2,1,0:T(8,128)} %all_to_all.14.parts, bf16[24,128,128]{2,1,0:T(8,128)(2,1)} %bitcast.20), custom_call_target="tpu_custom_call" | custom-call | tf_op jit(solution)/shard_map/pallas_call | solution.py:247
  (68 shorter events, 5.2 us)
Async XLA Ops:
  0.0 2.2 %copy-start.12 = (bf16[944,1024]{1,0:T(8,128)(2,1)S(1)}, bf16[944,1024]{1,0:T(8,128)(2,1)}, u32[]{:S(2)}) copy-start(bf16[944,1024]{1,0:T(8,128)(2,1)} %param.10) | copy-start | bytes 5799940
  0.0 2.2 %copy-start.13 = (bf16[944,472]{1,0:T(8,128)(2,1)S(1)}, bf16[944,472]{1,0:T(8,128)(2,1)}, u32[]{:S(2)}) copy-start(bf16[944,472]{1,0:T(8,128)(2,1)} %param.9) | copy-start | bytes 2673412
  8.8 10.7 %copy-start.10 = (s32[1024,8]{0,1:T(8,128)S(1)}, s32[1024,8]{0,1:T(8,128)}, u32[]{:S(2)}) copy-start(s32[1024,8]{0,1:T(8,128)} %param.7) | copy-start | bytes 98308
  8.8 10.7 %copy-start.11 = (s32[1024]{0:T(1024)S(1)}, s32[1024]{0:T(1024)}, u32[]{:S(2)}) copy-start(s32[1024]{0:T(1024)} %param.8) | copy-start | bytes 12292
  8.8 36.7 %all-to-all-start.1 = ((f32[32,14,8,128]{3,2,1,0:T(8,128)}), f32[32,14,8,128]{3,2,1,0:T(8,128)S(1)}, u32[]{:S(2)}, u32[]{:S(2)}) async-start(f32[32,14,8,128]{3,2,1,0:T(8,128)} %shard_map.55), calls=%async_computation.1 | async-start | bytes 3670016 | tf_op jit(solution)/shard_map/all_to_all | solution.py:180
  45.5 120.8 %copy-start = (f32[32,14,8,128]{3,2,1,0:T(8,128)}, f32[32,14,8,128]{3,2,1,0:T(8,128)S(1)}, u32[]{:S(2)}) copy-start(f32[32,14,8,128]{3,2,1,0:T(8,128)S(1)} %all-to-all-done.1) | copy-start | bytes 5505028
  49.1 38.7 %collective-permute-start = (f32[36,8,128]{2,1,0:T(8,128)}, f32[36,8,128]{2,1,0:T(8,128)S(1)}, u32[]{:S(2)}, u32[]{:S(2)}) collective-permute-start(f32[36,8,128]{2,1,0:T(8,128)} %get-tuple-element.41), channel_id=1, source_target_pairs={{0,128},{16,144},{32,160},{48,176},{64,192},{80,208},{96,224},{112... | collective-permute-start | bytes 442376 | tf_op jit(solution)/shard_map/ppermute | solution.py:212
  62.5 46.0 %collective-permute-start.1 = (f32[36,8,128]{2,1,0:T(8,128)}, f32[36,8,128]{2,1,0:T(8,128)S(1)}, u32[]{:S(2)}, u32[]{:S(2)}) collective-permute-start(f32[36,8,128]{2,1,0:T(8,128)} %get-tuple-element.42), channel_id=1, source_target_pairs={{0,112},{16,128},{32,144},{48,160},{64,176},{80,192},{96,208},{112... | collective-permute-start | bytes 442376 | tf_op jit(solution)/shard_map/ppermute | solution.py:212
  67.9 42.6 %collective-permute-start.2 = (f32[36,8,128]{2,1,0:T(8,128)}, f32[36,8,128]{2,1,0:T(8,128)S(1)}, u32[]{:S(2)}, u32[]{:S(2)}) collective-permute-start(f32[36,8,128]{2,1,0:T(8,128)} %get-tuple-element.43), channel_id=1, source_target_pairs={{0,144},{16,160},{32,176},{48,192},{64,208},{80,224},{96,240},{112... | collective-permute-start | bytes 442376 | tf_op jit(solution)/shard_map/ppermute | solution.py:212
  75.6 36.8 %collective-permute-start.3 = (f32[36,8,128]{2,1,0:T(8,128)}, f32[36,8,128]{2,1,0:T(8,128)S(1)}, u32[]{:S(2)}, u32[]{:S(2)}) collective-permute-start(f32[36,8,128]{2,1,0:T(8,128)} %get-tuple-element.44), channel_id=1, source_target_pairs={{0,96},{16,112},{32,128},{48,144},{64,160},{80,176},{96,192},{112,... | collective-permute-start | bytes 442376 | tf_op jit(solution)/shard_map/ppermute | solution.py:212
  80.5 39.2 %collective-permute-start.4 = (f32[36,8,128]{2,1,0:T(8,128)}, f32[36,8,128]{2,1,0:T(8,128)S(1)}, u32[]{:S(2)}, u32[]{:S(2)}) collective-permute-start(f32[36,8,128]{2,1,0:T(8,128)} %get-tuple-element.45), channel_id=1, source_target_pairs={{0,160},{16,176},{32,192},{48,208},{64,224},{80,240},{96,0},{112,1... | collective-permute-start | bytes 442376 | tf_op jit(solution)/shard_map/ppermute | solution.py:212
  87.8 78.6 %copy-start.1 = (f32[36,8,128]{2,1,0:T(8,128)}, f32[36,8,128]{2,1,0:T(8,128)S(1)}, u32[]{:S(2)}) copy-start(f32[36,8,128]{2,1,0:T(8,128)S(1)} %collective-permute-done.refs_1_) | copy-start | bytes 442372
  87.8 49.8 %collective-permute-start.5 = (f32[36,8,128]{2,1,0:T(8,128)}, f32[36,8,128]{2,1,0:T(8,128)S(1)}, u32[]{:S(2)}, u32[]{:S(2)}) collective-permute-start(f32[36,8,128]{2,1,0:T(8,128)} %get-tuple-element.46), channel_id=1, source_target_pairs={{0,80},{16,96},{32,112},{48,128},{64,144},{80,160},{96,176},{112,1... | collective-permute-start | bytes 442376 | tf_op jit(solution)/shard_map/ppermute | solution.py:212
  108.5 57.8 %copy-start.2 = (f32[36,8,128]{2,1,0:T(8,128)}, f32[36,8,128]{2,1,0:T(8,128)S(1)}, u32[]{:S(2)}) copy-start(f32[36,8,128]{2,1,0:T(8,128)S(1)} %collective-permute-done.1.refs_2_) | copy-start | bytes 442372
  108.5 31.0 %collective-permute-start.6 = (f32[36,8,128]{2,1,0:T(8,128)}, f32[36,8,128]{2,1,0:T(8,128)S(1)}, u32[]{:S(2)}, u32[]{:S(2)}) collective-permute-start(f32[36,8,128]{2,1,0:T(8,128)} %get-tuple-element.47), channel_id=1, source_target_pairs={{0,176},{16,192},{32,208},{48,224},{64,240},{80,0},{96,16},{112,32... | collective-permute-start | bytes 442376 | tf_op jit(solution)/shard_map/ppermute | solution.py:212
  110.4 55.9 %copy-start.3 = (f32[36,8,128]{2,1,0:T(8,128)}, f32[36,8,128]{2,1,0:T(8,128)S(1)}, u32[]{:S(2)}) copy-start(f32[36,8,128]{2,1,0:T(8,128)S(1)} %collective-permute-done.2.refs_3_) | copy-start | bytes 442372
  110.5 31.1 %collective-permute-start.7 = (f32[36,8,128]{2,1,0:T(8,128)}, f32[36,8,128]{2,1,0:T(8,128)S(1)}, u32[]{:S(2)}, u32[]{:S(2)}) collective-permute-start(f32[36,8,128]{2,1,0:T(8,128)} %get-tuple-element.48), channel_id=1, source_target_pairs={{0,64},{16,80},{32,96},{48,112},{64,128},{80,144},{96,160},{112,17... | collective-permute-start | bytes 442376 | tf_op jit(solution)/shard_map/ppermute | solution.py:212
  112.4 53.9 %copy-start.4 = (f32[36,8,128]{2,1,0:T(8,128)}, f32[36,8,128]{2,1,0:T(8,128)S(1)}, u32[]{:S(2)}) copy-start(f32[36,8,128]{2,1,0:T(8,128)S(1)} %collective-permute-done.3.refs_4_) | copy-start | bytes 442372
  112.4 34.6 %collective-permute-start.8 = (f32[36,8,128]{2,1,0:T(8,128)}, f32[36,8,128]{2,1,0:T(8,128)S(1)}, u32[]{:S(2)}, u32[]{:S(2)}) collective-permute-start(f32[36,8,128]{2,1,0:T(8,128)} %get-tuple-element.49), channel_id=1, source_target_pairs={{0,192},{16,208},{32,224},{48,240},{64,0},{80,16},{96,32},{112,48}... | collective-permute-start | bytes 442376 | tf_op jit(solution)/shard_map/ppermute | solution.py:212
  119.7 46.6 %copy-start.5 = (f32[36,8,128]{2,1,0:T(8,128)}, f32[36,8,128]{2,1,0:T(8,128)S(1)}, u32[]{:S(2)}) copy-start(f32[36,8,128]{2,1,0:T(8,128)S(1)} %collective-permute-done.4.refs_5_) | copy-start | bytes 442372
  119.7 35.1 %collective-permute-start.9 = (f32[36,8,128]{2,1,0:T(8,128)}, f32[36,8,128]{2,1,0:T(8,128)}, u32[]{:S(2)}, u32[]{:S(2)}) collective-permute-start(f32[36,8,128]{2,1,0:T(8,128)} %get-tuple-element.50), channel_id=1, source_target_pairs={{0,48},{16,64},{32,80},{48,96},{64,112},{80,128},{96,144},{112,160... | collective-permute-start | bytes 442376 | tf_op jit(solution)/shard_map/ppermute | solution.py:212
  137.6 28.7 %copy-start.6 = (f32[36,8,128]{2,1,0:T(8,128)}, f32[36,8,128]{2,1,0:T(8,128)S(1)}, u32[]{:S(2)}) copy-start(f32[36,8,128]{2,1,0:T(8,128)S(1)} %collective-permute-done.5.refs_6_) | copy-start | bytes 442372
  137.6 22.6 %collective-permute-start.10 = (f32[36,8,128]{2,1,0:T(8,128)}, f32[36,8,128]{2,1,0:T(8,128)}, u32[]{:S(2)}, u32[]{:S(2)}) collective-permute-start(f32[36,8,128]{2,1,0:T(8,128)} %get-tuple-element.51), channel_id=1, source_target_pairs={{0,208},{16,224},{32,240},{48,0},{64,16},{80,32},{96,48},{112,64},... | collective-permute-start | bytes 442376 | tf_op jit(solution)/shard_map/ppermute | solution.py:212
  139.6 26.8 %copy-start.7 = (f32[36,8,128]{2,1,0:T(8,128)}, f32[36,8,128]{2,1,0:T(8,128)S(1)}, u32[]{:S(2)}) copy-start(f32[36,8,128]{2,1,0:T(8,128)S(1)} %collective-permute-done.6.refs_7_) | copy-start | bytes 442372
  139.6 20.7 %collective-permute-start.11 = (f32[36,8,128]{2,1,0:T(8,128)}, f32[36,8,128]{2,1,0:T(8,128)}, u32[]{:S(2)}, u32[]{:S(2)}) collective-permute-start(f32[36,8,128]{2,1,0:T(8,128)} %get-tuple-element.52), channel_id=1, source_target_pairs={{0,32},{16,48},{32,64},{48,80},{64,96},{80,112},{96,128},{112,144}... | collective-permute-start | bytes 442376 | tf_op jit(solution)/shard_map/ppermute | solution.py:212
  141.5 24.8 %copy-start.8 = (f32[36,8,128]{2,1,0:T(8,128)}, f32[36,8,128]{2,1,0:T(8,128)S(1)}, u32[]{:S(2)}) copy-start(f32[36,8,128]{2,1,0:T(8,128)S(1)} %collective-permute-done.7.refs_8_) | copy-start | bytes 442372
  141.5 20.5 %collective-permute-start.12 = (f32[36,8,128]{2,1,0:T(8,128)}, f32[36,8,128]{2,1,0:T(8,128)}, u32[]{:S(2)}, u32[]{:S(2)}) collective-permute-start(f32[36,8,128]{2,1,0:T(8,128)} %get-tuple-element.53), channel_id=1, source_target_pairs={{0,224},{16,240},{32,0},{48,16},{64,32},{80,48},{96,64},{112,80},{... | collective-permute-start | bytes 442376 | tf_op jit(solution)/shard_map/ppermute | solution.py:212
  147.0 19.4 %copy-start.9 = (f32[36,8,128]{2,1,0:T(8,128)}, f32[36,8,128]{2,1,0:T(8,128)S(1)}, u32[]{:S(2)}) copy-start(f32[36,8,128]{2,1,0:T(8,128)S(1)} %collective-permute-done.8.refs_9_) | copy-start | bytes 442372
  147.0 16.7 %collective-permute-start.13 = (f32[36,8,128]{2,1,0:T(8,128)}, f32[36,8,128]{2,1,0:T(8,128)}, u32[]{:S(2)}, u32[]{:S(2)}) collective-permute-start(f32[36,8,128]{2,1,0:T(8,128)} %get-tuple-element.54), channel_id=1, source_target_pairs={{0,16},{16,32},{32,48},{48,64},{64,80},{80,96},{96,112},{112,128},... | collective-permute-start | bytes 442376 | tf_op jit(solution)/shard_map/ppermute | solution.py:212
  154.8 11.5 %collective-permute-start.14 = (f32[36,8,128]{2,1,0:T(8,128)}, f32[36,8,128]{2,1,0:T(8,128)}, u32[]{:S(2)}, u32[]{:S(2)}) collective-permute-start(f32[36,8,128]{2,1,0:T(8,128)} %get-tuple-element.55), channel_id=1, source_target_pairs={{0,240},{16,0},{32,16},{48,32},{64,48},{80,64},{96,80},{112,96},{1... | collective-permute-start | bytes 442376 | tf_op jit(solution)/shard_map/ppermute | solution.py:212

commit v3 on v1

v3 whole, which is shorter than its diff:
```python
import functools

import jax
import jax.numpy as jnp
from jax import lax
from jax.experimental import pallas as pl
from jax.experimental.pallas import tpu as pltpu
from jax.sharding import Mesh, PartitionSpec as P

CS = 2
YLO, NZ, XS, YHI, CORE = 2, 16, 4, 2, 2
NCOL = XS * YHI * CORE
PLANE = ("ylo", "x", "yhi", "core")
NPLANE = YLO * NCOL
LIVE = 6
SLOTS = 2 * LIVE + CS
NQ = 24
CAP = 22
NEAR = 44
LOCAL = 40
FULL = 64
AHEAD = 8
FARTHEST = AHEAD - 1
TRASH = NPLANE * NQ
VMEM = pl.BlockSpec(memory_space=pltpu.VMEM)
SMEM = pl.BlockSpec(memory_space=pltpu.SMEM)


def kernel_call(kernel, limit=16, **rest):
    params = pltpu.CompilerParams(vmem_limit_bytes=limit * 2**20)
    return pl.pallas_call(kernel, compiler_params=params, **rest)


def low_half(shape):
    return lax.broadcasted_iota(jnp.int32, shape, 0) % 8 < 4


def slice_kernel(first, second, out):
    low = low_half((128, 128))

    def put(slot, left, right):
        even = jnp.where(low, left, jnp.roll(right.reshape(16, 8, 128), 4, axis=1).reshape(128, 128))
        odd = jnp.where(low, jnp.roll(left.reshape(16, 8, 128), 4, axis=1).reshape(128, 128), right)
        even = even.reshape(16, 8, 128)
        odd = odd.reshape(16, 8, 128)
        for i in range(16):
            out[2 * i, slot] = even[i]
            out[2 * i + 1, slot] = odd[i]

    for member, tiles in enumerate((first, second)):
        for k in range(LIVE):
            rows = pl.ds((CS + k) * 128, 128)
            put(member * LIVE + k, tiles[rows, 0:128], tiles[rows, 128:256])
    for k in range(CS):
        rows = pl.ds(k * 128, 128)
        put(
            2 * LIVE + k,
            first[rows, 0:128] + second[rows, 0:128],
            first[rows, 128:256] + second[rows, 128:256],
        )


def offset_of(code):
    return code + 1 if code < AHEAD else AHEAD - 1 - code


def shared_slice(slices, target, k):
    source = lax.rem(target + NZ - k, NZ)
    return (
        slices[source * SLOTS + 2 * LIVE + k]
        + slices[(NCOL + source) * SLOTS + 2 * LIVE + k]
    )


def add_rows(count, list_ref, base, src, total):
    def body(p, carry):
        spot = list_ref[base + p]
        total[spot] = total[spot] + src[p]
        return carry

    lax.fori_loop(0, count, body, 0, unroll=2)


def pack_kernel(meta, send_list, slices, out):
    me = meta[0]
    for code in range(NZ - 1):
        target = lax.rem(me + offset_of(code) + NZ, NZ)
        base = target * (CAP + CS)

        def body(p, carry, code=code, base=base):
            out[base + p] = slices[send_list[code * LOCAL + p]]
            return carry

        lax.fori_loop(0, CAP, body, 0, unroll=2)
        for k in range(CS):
            out[base + CAP + k] = shared_slice(slices, target, k)


def relay_kernel(meta, push, kept, send_list, slices, buf, ahead, behind):
    me = meta[0]
    for first, last, row, out in ((0, 8, 16, ahead), (8, 15, 17, behind)):
        step = -1 if first == 0 else 1
        count = push[first]
        base = row * LOCAL

        def own(p, carry, base=base, out=out):
            out[p] = slices[send_list[base + p]]
            return carry

        lax.fori_loop(0, jnp.minimum(count, LOCAL), own, 0)
        for code in range(first + 1, last):
            line = (step * (code - first)) % NZ
            begin = kept[line * NZ + code - 1] + lax.rem(me + line, NZ) * (CAP + CS)
            more = push[line * NZ + code]

            def body(p, carry, out=out, begin=begin, count=count):
                out[count + p] = buf[begin + p]
                return carry

            lax.fori_loop(0, more, body, 0)
            count = count + more


def early_kernel(meta, recv_list, send_list, slices, buf, total):
    me = meta[0]
    total[...] = jnp.zeros_like(total)

    def body(p, carry):
        spot = recv_list[p]
        total[spot] = total[spot] + slices[send_list[15 * LOCAL + p]]
        return carry

    lax.fori_loop(0, LOCAL, body, 0, unroll=2)
    tiles = [shared_slice(slices, me, k) for k in range(CS)]
    for line in range(1, NZ):
        base = lax.rem(me + line, NZ) * (CAP + CS)

        def add(p, carry, base=base, line=line):
            spot = recv_list[line * LOCAL + p]
            total[spot] = total[spot] + buf[base + p]
            return carry

        lax.fori_loop(0, CAP, add, 0, unroll=2)
        tiles = [tile + buf[base + CAP + k] for k, tile in enumerate(tiles)]
    for k in range(CS):
        spot = lax.rem(me + NZ - k, NZ) * NQ
        total[spot] = total[spot] + tiles[k]


def merge(total, out):
    low = low_half((8, 128))

    def body(at, carry):
        side = at // NCOL * NCOL
        left = lax.rem(at + NCOL - 1, NCOL) + side
        for h in range(NQ // 2):
            a0 = total[at * NQ + 2 * h]
            a1 = total[at * NQ + 2 * h + 1]
            b0 = total[left * NQ + 2 * h]
            b1 = total[left * NQ + 2 * h + 1]
            out[at, h] = jnp.where(
                low, a0 + jnp.roll(b0, 4, axis=0), jnp.roll(a1, 4, axis=0) + b1
            )
        return carry

    lax.fori_loop(0, NPLANE, body, 0)


def late_kernel(near_list, ahead, behind, early, out, total):
    total[...] = early[...]
    add_rows(NEAR, near_list, 0, ahead, total)
    add_rows(NEAR, near_list, NEAR, behind, total)
    merge(total, out)


def full_pack_kernel(send_list, slices, out):
    def body(target, carry):
        def inner(p, carry):
            out[target * (FULL + CS) + p] = slices[send_list[target * FULL + p]]
            return carry

        lax.fori_loop(0, FULL, inner, 0)
        for k in range(CS):
            out[target * (FULL + CS) + FULL + k] = shared_slice(slices, target, k)
        return carry

    lax.fori_loop(0, NZ, body, 0)


def full_gather_kernel(meta, recv_list, buf, out, total):
    me = meta[0]
    total[...] = jnp.zeros_like(total)

    def body(source, carry):
        def inner(p, carry):
            spot = recv_list[source * FULL + p]
            total[spot] = total[spot] + buf[source * (FULL + CS) + p]
            return carry

        lax.fori_loop(0, FULL, inner, 0)
        for k in range(CS):
            spot = lax.rem(me + NZ - k, NZ) * NQ
            total[spot] = total[spot] + buf[source * (FULL + CS) + FULL + k]
        return carry

    lax.fori_loop(0, NZ, body, 0)
    merge(total, out)


def final_kernel(parts, given, out):
    low = low_half((8, 128))

    def body(h, carry):
        for half in range(2):
            base = given[2 * h + half].astype(jnp.float32)
            for i in range(16):
                a = parts[2 * i, h]
                b = parts[2 * i + 1, h]
                if half == 0:
                    tile = jnp.where(low, a, jnp.roll(b, 4, axis=0))
                else:
                    tile = jnp.where(low, jnp.roll(a, 4, axis=0), b)
                out[2 * h + half, 8 * i : 8 * i + 8, :] = base[8 * i : 8 * i + 8] - tile
        return carry

    lax.fori_loop(0, NQ // 2, body, 0)


def lists_of(spots, value, count):
    at = jnp.arange(count, dtype=jnp.int32)
    return jnp.sum(
        jnp.where(spots[:, None, :] == at[None, :, None], value[:, None, :], 0), axis=-1
    )


def shape_of(*shape):
    return jax.ShapeDtypeStruct(shape, jnp.float32)


MERGED = shape_of(NPLANE, NQ // 2, 8, 128)
TOTAL = pltpu.VMEM((TRASH + 1, 8, 128), jnp.float32)


def ranks_of(mask, before):
    rank = jnp.dot(mask.astype(jnp.bfloat16), before, preferred_element_type=jnp.float32)
    return rank.astype(jnp.int32)


def on_device(block_ids, iface_counts, inv_factor, coupling, boundary_block):
    me = lax.axis_index("z").astype(jnp.int32)
    width = inv_factor.shape[1]
    tiles = []
    for member in range(2):
        rows = slice(member * width, (member + 1) * width)
        mixed = jnp.dot(
            inv_factor[rows], coupling[rows], preferred_element_type=jnp.float32
        ).astype(jnp.bfloat16)
        tiles.append(
            lax.dot_general(
                mixed,
                mixed[:, : CS * 128],
                (((0,), (0,)), ((), ())),
                preferred_element_type=jnp.float32,
            )
        )
    slices = kernel_call(
        slice_kernel,
        out_shape=shape_of(NPLANE, SLOTS, 8, 128),
        in_specs=[VMEM, VMEM],
        out_specs=VMEM,
    )(*tiles)
    spread = lax.all_to_all(slices, PLANE, 0, 0, tiled=True).reshape(NPLANE * SLOTS, 8, 128)

    slot = jnp.arange(8, dtype=jnp.int32)
    alive = (slot[None] >= CS) & (slot[None] < iface_counts[:, None])
    key = jnp.where(alive, block_ids, -1)
    key = key.reshape(YLO, NZ, NCOL * 16).transpose(1, 0, 2).reshape(NZ, NPLANE * 16)
    key = lax.dynamic_slice_in_dim(jnp.concatenate([key, key], axis=0), me, NZ, 0)
    entry = jnp.arange(NPLANE * 16, dtype=jnp.int32)
    before = (entry[:, None] < entry[None, :]).astype(jnp.bfloat16)
    step = jnp.arange(NZ, dtype=jnp.int32)
    line, code = step[:, None], step[None, :]
    spot = (((key >> 4) & 1) * NCOL + ((entry >> 4) & 15)[None]) * NQ + (key >> 5) - TRASH
    origin = (entry >> 4) * SLOTS + ((entry >> 3) & 1) * LIVE + (entry & 7) - CS
    dead = key < 0
    hop = (key - me - line) & 15
    turn = jnp.where(hop == 0, 15, jnp.where(hop <= AHEAD, hop - 1, 23 - hop))
    turn = jnp.where(dead, -1, turn)
    load = jnp.sum((turn[:, None, :] == step[None, :, None]).astype(jnp.int32), axis=-1)

    inner = (step[:, None] // AHEAD == step[None, :] // AHEAD) & (step[None, :] >= step[:, None])
    extra = jnp.where(code == 15, 0, load) - CAP
    run = jnp.sum(jnp.where(inner[None], extra[:, None, :], 0), axis=-1)
    push = run - jnp.minimum(jnp.min(jnp.where(inner[None], run[:, None, :], 0), axis=-1), 0)
    kept = load - push
    place = step[:, None, None]
    lag = jnp.where(step < AHEAD, -step, step - AHEAD)[None, None, :]
    meets = ((place + lag - step[None, :, None]) & 15) == 0
    near = jnp.where(meets, push[None], 0)
    near_ahead = jnp.sum(jnp.where(code[None] < AHEAD, near, 0), axis=(1, 2))
    near_behind = jnp.sum(jnp.where(code[None] < AHEAD, 0, near), axis=(1, 2))
    crowded = (
        (jnp.min(kept) < 0)
        | (jnp.max(near_ahead) > NEAR)
        | (jnp.max(near_behind) > NEAR)
        | (jnp.max(push) > LOCAL)
        | (jnp.max(jnp.where(code == 15, load, 0)) > LOCAL)
    )

    mine = (key & 15 == me) & ~dead
    sent = turn[0][None] == step[:, None]
    rank = ranks_of(jnp.concatenate([mine, sent], axis=0), before)
    rank_mine, rank_sent = rank[:NZ], rank[NZ:]
    own_code = jnp.where(line == 0, 15, jnp.where(line < 8, 7 + line, 15 - line))
    push_mine = jnp.sum(jnp.where(code == own_code, push, 0), axis=1)
    spots_mine = jnp.where(mine, rank_mine - push_mine[:, None], -1)
    sooner = (line // 8 == code // 8) & jnp.where(line < 8, code < line, code > line)
    base = jnp.sum(jnp.where(sooner, push_mine[None], 0), axis=1)
    spots_near = jnp.where(
        mine & (rank_mine < push_mine[:, None]), base[:, None] + rank_mine, -1
    )
    push_own = push[0][:, None]
    stay = jnp.where(sent & (rank_sent >= push_own), rank_sent - push_own, -1)
    moved = jnp.where(sent & (rank_sent < push_own), rank_sent, -1)
    above = jnp.concatenate([moved[1:], moved[:1]], axis=0)
    rides = (above >= 0) & (line != FARTHEST) & (line < 14)
    spots_sent = jnp.where(rides, kept[0][:, None] + above, stay)
    table = lists_of(
        jnp.concatenate([spots_mine, spots_sent, moved[:1], moved[8:9]], axis=0),
        jnp.concatenate([spot, jnp.broadcast_to(origin[None], (NZ + 2, NPLANE * 16))], axis=0),
        LOCAL,
    )
    recv_list = (table[:NZ] + TRASH).reshape(-1)
    send_list = table[NZ:].reshape(-1)
    at = jnp.arange(NEAR, dtype=jnp.int32)[:, None, None]
    near_hits = jnp.where(spots_near[None] == at, spot[None], 0)
    near_list = (
        jnp.stack([jnp.sum(near_hits[:, 8:], axis=(1, 2)), jnp.sum(near_hits[:, :8], axis=(1, 2))])
        + TRASH
    ).reshape(-1)
    push_flat, kept_flat = push.reshape(-1), kept.reshape(-1)
    recv_list, send_list, near_list, push_flat, kept_flat, crowded = lax.optimization_barrier(
        (recv_list, send_list, near_list, push_flat, kept_flat, crowded)
    )
    meta = me.reshape(1)

    def fast(spread):
        buf = kernel_call(
            pack_kernel,
            out_shape=shape_of(NZ * (CAP + CS), 8, 128),
            in_specs=[SMEM, SMEM, VMEM],
            out_specs=VMEM,
        )(meta, send_list, spread)
        buf = lax.all_to_all(buf, "z", 0, 0, tiled=True)
        ahead, behind = kernel_call(
            relay_kernel,
            out_shape=[shape_of(NEAR, 8, 128)] * 2,
            in_specs=[SMEM] * 4 + [VMEM] * 2,
            out_specs=[VMEM] * 2,
        )(meta, push_flat, kept_flat, send_list, spread, buf)
        ahead = lax.ppermute(ahead, "z", [(i, (i + 1) % NZ) for i in range(NZ)])
        behind = lax.ppermute(behind, "z", [(i, (i - 1) % NZ) for i in range(NZ)])
        total = kernel_call(
            early_kernel,
            out_shape=shape_of(TRASH + 1, 8, 128),
            in_specs=[SMEM] * 3 + [VMEM] * 2,
            out_specs=VMEM,
        )(meta, recv_list, send_list, spread, buf)
        return kernel_call(
            late_kernel,
            out_shape=MERGED,
            in_specs=[SMEM] + [VMEM] * 3,
            out_specs=VMEM,
            scratch_shapes=[TOTAL],
        )(near_list, ahead, behind, total)

    def full(spread):
        plane = jnp.where(dead, NZ, key & 15)
        mask = jnp.concatenate([mine, plane[0][None] == step[:, None]], axis=0)
        spots = jnp.where(mask, ranks_of(mask, before), -1)
        value = jnp.concatenate([spot, jnp.broadcast_to(origin[None], spot.shape)], axis=0)
        lists = lists_of(spots, value, FULL)
        theirs = lists[NZ:].reshape(-1)
        ours = (jnp.roll(lists[:NZ], me, axis=0) + TRASH).reshape(-1)
        buf = kernel_call(
            full_pack_kernel,
            out_shape=shape_of(NZ * (FULL + CS), 8, 128),
            in_specs=[SMEM, VMEM],
            out_specs=VMEM,
        )(theirs, spread)
        buf = lax.all_to_all(buf, "z", 0, 0, tiled=True)
        return kernel_call(
            full_gather_kernel,
            out_shape=MERGED,
            in_specs=[SMEM, SMEM, VMEM],
            out_specs=VMEM,
            scratch_shapes=[TOTAL],
        )(meta, ours, buf)

    merged = lax.cond(crowded, full, fast, spread)
    parts = lax.all_to_all(merged, PLANE, 0, 0, tiled=True)
    result = kernel_call(
        final_kernel,
        out_shape=shape_of(NQ, 128, 128),
        in_specs=[VMEM, VMEM],
        out_specs=VMEM,
    )(parts, boundary_block.reshape(NQ, 128, 128))
    return result.reshape(NQ, 128, 1, 128)


def solution(mesh):
    fine = Mesh(mesh.devices.reshape(YLO, NZ, XS, YHI, CORE), ("ylo", "z", "x", "yhi", "core"))
    row, col = ("ylo", "z"), ("x", "yhi", "core")
    return jax.shard_map(
        on_device,
        mesh=fine,
        in_specs=(
            P(),
            P(),
            P(row + col, None),
            P(row + col, None),
            P(None, row, None, col),
        ),
        out_specs=P(None, row, None, col),
        check_vma=False,
    )
```

time: 243 us -> 174 us (0.72)
  starting transfers between devices: 110 us -> 20.1 us
  blocking collectives: 28.9 us -> 113 us
  waiting for transfers between devices: 74.4 us -> 13 us
  other arithmetic: 1.97 us -> 8.39 us
  Pallas kernels: 16.3 us -> 10.4 us
  between operations: 1.14 us -> 3.59 us
    ppermute x15 -> x2, starting transfers between devices: 99.2 us -> 9.43 us  [the longest x1 4.93 us: fast(): ahead = lax.ppermute(ahead, 'z', [(i, (i + 1) % NZ) for i in range(NZ)])]
    all_to_all x0 -> x1, blocking collectives: none -> 80.4 us  [fast(): buf = lax.all_to_all(buf, 'z', 0, 0, tiled=True)]
    ppermute x15 -> x2, waiting for transfers between devices: 51.9 us -> 0.01 us  [the longest x1 0.01 us: fast(): ahead = lax.ppermute(ahead, 'z', [(i, (i + 1) % NZ) for i in range(NZ)])]
    all_to_all x1, waiting for transfers between devices: 22.5 us -> 13 us  [on_device(): lax.all_to_all(slices, PLANE, 0, 0, tiled=True)]
    pallas_call x5 -> x6, Pallas kernels: 16.3 us -> 10.4 us  [the longest x1 2.92 us: fast(): kernel_call(early_kernel, out_shape=shape_of(TRASH + 1, 8, 128), in_specs...]
    all_to_all x1, blocking collectives: 28.9 us -> 33 us  [on_device(): parts = lax.all_to_all(merged, PLANE, 0, 0, tiled=True)]
    reduce_sum x2 -> x6, other arithmetic: 1.04 us -> 3.87 us  [the longest x1 1.67 us: on_device(): jnp.sum(near_hits[:, 8:], axis=(1, 2))]
  transfers between devices with their start and end apart: 16 -> 3, of which waited for: 8 -> 1; matrix products, arithmetic and copies ran while one was open for 2% -> 5% of each run, Pallas kernels for 0% -> 2%
where the time goes in v3:
time: 174 us
  blocking collectives  113 us (65%)
  starting transfers between devices  20.1 us (12%)
  waiting for transfers between devices  13 us (7%)
  Pallas kernels  10.4 us (6%)
  other arithmetic  8.39 us (5%)
  matrix products  4.01 us (2%)
  between operations  3.59 us (2%)
    all_to_all x1, blocking collectives, fast(): buf = lax.all_to_all(buf, 'z', 0, 0, tiled=True)  80.4 us
    all_to_all x1, blocking collectives, on_device(): parts = lax.all_to_all(merged, PLANE, 0, 0, tiled=True)  33 us
    all_to_all x1, waiting for transfers between devices, on_device(): lax.all_to_all(slices, PLANE, 0, 0, tiled=True)  13 us
    all_to_all x1, starting transfers between devices, on_device(): lax.all_to_all(slices, PLANE, 0, 0, tiled=True)  10.7 us
    ppermute x1, starting transfers between devices, fast(): ahead = lax.ppermute(ahead, 'z', [(i, (i + 1) % NZ) for i in range(NZ)])  4.93 us
    ppermute x1, starting transfers between devices, fast(): behind = lax.ppermute(behind, 'z', [(i, (i - 1) % NZ) for i in range(NZ)])  4.5 us
  transfers between devices with their start and end apart: 3, of which 1 were waited for; matrix products, arithmetic and copies ran while one was open for 5% of the time, Pallas kernels for 2%

profile of v3, /device:TPU:1, one launch (start us, length us, event | category | flops | bytes accessed | tf_op | source)
XLA Modules:
  0.0 174.0 jit_solution(6768789802089340101)
XLA Ops:
  0.0 2.2 %convolution_convert_fusion.1 = bf16[472,1024]{1,0:T(8,128)(2,1)S(1)} fusion(bf16[944,1024]{1,0:T(8,128)(2,1)} %param.10, bf16[944,472]{1,0:T(8,128)(2,1)} %param.9), kind=kOutput, calls=%fused_computation.19 | convolution fusion | flops 456744960 | bytes 2416640 | tf_op jit(solution)/shard_map/dot_general | solution.py:255
  2.2 0.7 convolution_convert_fusion.2
  2.9 0.5 fusion.13.second
  3.4 0.5 fusion.15.first
  3.9 1.4 shard_map.55
  5.3 10.7 %all-to-all-start.2 = ((f32[32,14,8,128]{3,2,1,0:T(8,128)}), f32[32,14,8,128]{3,2,1,0:T(8,128)S(1)}, u32[]{:S(2)}, u32[]{:S(2)}) async-start(f32[32,14,8,128]{3,2,1,0:T(8,128)} %shard_map.55), calls=%async_computation.2 | async-start | bytes 3670016 | tf_op jit(solution)/shard_map/all_to_all | solution.py:272
  16.1 0.2 copy.10
  16.3 0.3 reshape.290
  16.7 0.4 convert_reduce_fusion
  17.2 0.6 select_reduce_fusion.4
  17.8 0.3 select_reduce_fusion.3
  18.2 0.3 select_reduce_fusion.2
  18.5 0.7 fusion.38
  19.2 0.7 fusion.36
  20.0 0.7 fusion.18
  20.6 0.2 select_reduce_fusion.5
  20.8 0.2 convolution_convert_fusion.3
  22.0 0.7 reduce_max.36
  22.7 0.7 reduce_max.37
  26.1 0.7 select_reduce_fusion.1
  27.2 1.7 slice_reduce_fusion.1
  29.0 13.0 %all-to-all-done.2 = f32[32,14,8,128]{3,2,1,0:T(8,128)S(1)} async-done(((f32[32,14,8,128]{3,2,1,0:T(8,128)}), f32[32,14,8,128]{3,2,1,0:T(8,128)S(1)}, u32[]{:S(2)}, u32[]{:S(2)}) %all-to-all-start.2) | async-done | bytes 1835040 | tf_op jit(solution)/shard_map/all_to_all | solution.py:272
  42.0 97.5 %conditional.1 = (f32[32,12,8,128]{3,2,1,0:T(8,128)S(1)}) conditional(s32[]{:T(128)} %convert_element_type.25, (s32[1]{0:T(128)}, s32[720]{0:T(1024)S(1)}, f32[448,8,128]{2,1,0:T(8,128)S(1)}, s32[256]{0:T(256)S(1)}, s32[256]{0:T(256)S(1)}, /*index=5*/s32[640]{0:T(1024)S(1)}, s32[88]{0:T(128)S(1)}) %tuple.31, (s32[16,512]{1,0:T(8,128)S(1)}, ...), branch_computations={%region_15.16_spmd, %region_16.18_spmd} | conditional | flops 20018704 | bytes 31249188 | solution.py:400
  42.0 1.9 %branch_0_fun.4 = f32[384,8,128]{2,1,0:T(8,128)S(1)} custom-call(s32[1]{0:T(128)} %get-tuple-element.68.meta, s32[720]{0:T(1024)S(1)} %get-tuple-element.71.send_list, f32[448,8,128]{2,1,0:T(8,128)S(1)} %get-tuple-element.72.slices), custom_call_target="tpu_custom_call" | custom-call | tf_op jit(solution)/shard_map/cond/branch_0_fun/pallas_call | solution.py:348
  43.9 80.4 %all_to_all.18.buf = f32[384,8,128]{2,1,0:T(8,128)S(1)} all-to-all(f32[384,8,128]{2,1,0:T(8,128)S(1)} %branch_0_fun.4), channel_id=1, replica_groups=mesh['ylo'=2,'z'=16,'x'=4,'yhi'=2,'core'=2] {'z'}, dimensions={0} | all-to-all | bytes 3145728 | tf_op jit(solution)/shard_map/cond/branch_0_fun/all_to_all | solution.py:354
  124.4 0.9 branch_0_fun.5
  125.2 4.9 %collective-permute-start = (f32[44,8,128]{2,1,0:T(8,128)S(1)}, f32[44,8,128]{2,1,0:T(8,128)S(1)}, u32[]{:S(2)}, u32[]{:S(2)}) collective-permute-start(f32[44,8,128]{2,1,0:T(8,128)S(1)} %get-tuple-element.73), channel_id=1, source_target_pairs={{0,16},{16,32},{32,48},{48,64},{64,80},{80,96},{96,112},{112,128},... | collective-permute-start | bytes 540680 | tf_op jit(solution)/shard_map/cond/branch_0_fun/ppermute | solution.py:361
  130.2 4.5 %collective-permute-start.1 = (f32[44,8,128]{2,1,0:T(8,128)S(1)}, f32[44,8,128]{2,1,0:T(8,128)S(1)}, u32[]{:S(2)}, u32[]{:S(2)}) collective-permute-start(f32[44,8,128]{2,1,0:T(8,128)S(1)} %get-tuple-element.74), channel_id=1, source_target_pairs={{0,240},{16,0},{32,16},{48,32},{64,48},{80,64},{96,80},{112,96},{1... | collective-permute-start | bytes 540680 | tf_op jit(solution)/shard_map/cond/branch_0_fun/ppermute | solution.py:362
  134.7 2.9 %branch_0_fun.6.early = f32[769,8,128]{2,1,0:T(8,128)S(1)} custom-call(s32[1]{0:T(128)} %get-tuple-element.68.meta, s32[640]{0:T(1024)S(1)} %get-tuple-element.75.recv_list, s32[720]{0:T(1024)S(1)} %get-tuple-element.71.send_list, f32[448,8,128]{2,1,0:T(8,128)S(1)} %get-tuple-element.72.slices, f32[384,8,128]{2,1,0:T(8,128)S(1)} %all_to_all.18.buf), custom_call_target="tpu_custom_call" | custom-call | tf_op jit(solution)/shard_map/cond/branch_0_fun/pallas_call | solution.py:363
  137.6 1.8 %branch_0_fun.7 = f32[32,12,8,128]{3,2,1,0:T(8,128)S(1)} custom-call(s32[88]{0:T(128)S(1)} %get-tuple-element.67.near_list, f32[44,8,128]{2,1,0:T(8,128)S(1)} %collective-permute-done.ahead, f32[44,8,128]{2,1,0:T(8,128)S(1)} %collective-permute-done.1.behind, f32[769,8,128]{2,1,0:T(8,128)S(1)} %branch_0_fun.6.early), custom_call_target="tpu_custom_call" | custom-call | tf_op jit(solution)/shard_map/cond/branch_0_fun/pallas_call | solution.py:369
  139.5 33.0 %all_to_all.19.parts = f32[32,12,8,128]{3,2,1,0:T(8,128)S(1)} all-to-all(f32[32,12,8,128]{3,2,1,0:T(8,128)S(1)} %get-tuple-element.124), channel_id=1, replica_groups=mesh['ylo'=2,'z'=16,'x'=4,'yhi'=2,'core'=2] {'ylo','x','yhi','core'}, dimensions={0} | all-to-all | bytes 3145728 | tf_op jit(solution)/shard_map/all_to_all | solution.py:401
  172.5 1.5 shard_map.56
  (51 shorter events, 1.2 us)
Async XLA Ops:
  0.0 2.2 %copy-start.4 = (bf16[944,1024]{1,0:T(8,128)(2,1)S(1)}, bf16[944,1024]{1,0:T(8,128)(2,1)}, u32[]{:S(2)}) copy-start(bf16[944,1024]{1,0:T(8,128)(2,1)} %param.10) | copy-start | bytes 5799940
  0.0 2.2 %copy-start.5 = (bf16[944,472]{1,0:T(8,128)(2,1)S(1)}, bf16[944,472]{1,0:T(8,128)(2,1)}, u32[]{:S(2)}) copy-start(bf16[944,472]{1,0:T(8,128)(2,1)} %param.9) | copy-start | bytes 2673412
  5.3 10.8 %copy-start.2 = (s32[1024,8]{0,1:T(8,128)S(1)}, s32[1024,8]{0,1:T(8,128)}, u32[]{:S(2)}) copy-start(s32[1024,8]{0,1:T(8,128)} %param.7) | copy-start | bytes 98308
  5.3 10.8 %copy-start.3 = (s32[1024]{0:T(1024)S(1)}, s32[1024]{0:T(1024)}, u32[]{:S(2)}) copy-start(s32[1024]{0:T(1024)} %param.8) | copy-start | bytes 12292
  5.3 36.7 %all-to-all-start.2 = ((f32[32,14,8,128]{3,2,1,0:T(8,128)}), f32[32,14,8,128]{3,2,1,0:T(8,128)S(1)}, u32[]{:S(2)}, u32[]{:S(2)}) async-start(f32[32,14,8,128]{3,2,1,0:T(8,128)} %shard_map.55), calls=%async_computation.2 | async-start | bytes 3670016 | tf_op jit(solution)/shard_map/all_to_all | solution.py:272
  125.2 12.4 %collective-permute-start = (f32[44,8,128]{2,1,0:T(8,128)S(1)}, f32[44,8,128]{2,1,0:T(8,128)S(1)}, u32[]{:S(2)}, u32[]{:S(2)}) collective-permute-start(f32[44,8,128]{2,1,0:T(8,128)S(1)} %get-tuple-element.73), channel_id=1, source_target_pairs={{0,16},{16,32},{32,48},{48,64},{64,80},{80,96},{96,112},{112,128},... | collective-permute-start | bytes 540680 | tf_op jit(solution)/shard_map/cond/branch_0_fun/ppermute | solution.py:361
  130.2 7.4 %collective-permute-start.1 = (f32[44,8,128]{2,1,0:T(8,128)S(1)}, f32[44,8,128]{2,1,0:T(8,128)S(1)}, u32[]{:S(2)}, u32[]{:S(2)}) collective-permute-start(f32[44,8,128]{2,1,0:T(8,128)S(1)} %get-tuple-element.74), channel_id=1, source_target_pairs={{0,240},{16,0},{32,16},{48,32},{64,48},{80,64},{96,80},{112,96},{1... | collective-permute-start | bytes 540680 | tf_op jit(solution)/shard_map/cond/branch_0_fun/ppermute | solution.py:362
  139.5 33.0 %copy-start.1 = (bf16[24,128,1,128]{3,1,2,0:T(8,128)(2,1)S(1)}, bf16[24,128,1,128]{3,1,2,0:T(8,128)(2,1)}, u32[]{:S(2)}) copy-start(bf16[24,128,1,128]{3,1,2,0:T(8,128)(2,1)} %param.11) | copy-start | bytes 2359300

commit v4 on v3

--- a/solution.py
+++ b/solution.py
@@ -16,11 +16,9 @@
 SLOTS = 2 * LIVE + CS
 NQ = 24
 CAP = 22
-NEAR = 44
+NEAR = 64
 LOCAL = 40
 FULL = 64
-AHEAD = 8
-FARTHEST = AHEAD - 1
 TRASH = NPLANE * NQ
 VMEM = pl.BlockSpec(memory_space=pltpu.VMEM)
 SMEM = pl.BlockSpec(memory_space=pltpu.SMEM)
@@ -60,10 +58,6 @@
         )
 
 
-def offset_of(code):
-    return code + 1 if code < AHEAD else AHEAD - 1 - code
-
-
 def shared_slice(slices, target, k):
     source = lax.rem(target + NZ - k, NZ)
     return (
@@ -72,56 +66,44 @@
     )
 
 
-def add_rows(count, list_ref, base, src, total):
-    def body(p, carry):
-        spot = list_ref[base + p]
-        total[spot] = total[spot] + src[p]
-        return carry
-
-    lax.fori_loop(0, count, body, 0, unroll=2)
-
-
 def pack_kernel(meta, send_list, slices, out):
     me = meta[0]
     for code in range(NZ - 1):
-        target = lax.rem(me + offset_of(code) + NZ, NZ)
+        target = lax.rem(me + code + 1, NZ)
         base = target * (CAP + CS)
 
         def body(p, carry, code=code, base=base):
             out[base + p] = slices[send_list[code * LOCAL + p]]
             return carry
 
-        lax.fori_loop(0, CAP, body, 0, unroll=2)
+        lax.fori_loop(0, CAP, body, 0, unroll=True)
         for k in range(CS):
             out[base + CAP + k] = shared_slice(slices, target, k)
 
 
-def relay_kernel(meta, push, kept, send_list, slices, buf, ahead, behind):
+def relay_kernel(meta, push, kept, send_list, slices, buf, out):
     me = meta[0]
-    for first, last, row, out in ((0, 8, 16, ahead), (8, 15, 17, behind)):
-        step = -1 if first == 0 else 1
-        count = push[first]
-        base = row * LOCAL
-
-        def own(p, carry, base=base, out=out):
-            out[p] = slices[send_list[base + p]]
+    count = push[0]
+
+    def own(p, carry):
+        out[p] = slices[send_list[NZ * LOCAL + p]]
+        return carry
+
+    lax.fori_loop(0, count, own, 0)
+    for code in range(1, NZ - 1):
+        line = NZ - code
+        begin = kept[line * NZ + code - 1] + lax.rem(me + line, NZ) * (CAP + CS)
+        more = push[line * NZ + code]
+
+        def body(p, carry, begin=begin, count=count):
+            out[count + p] = buf[begin + p]
             return carry
 
-        lax.fori_loop(0, jnp.minimum(count, LOCAL), own, 0)
-        for code in range(first + 1, last):
-            line = (step * (code - first)) % NZ
-            begin = kept[line * NZ + code - 1] + lax.rem(me + line, NZ) * (CAP + CS)
-            more = push[line * NZ + code]
-
-            def body(p, carry, out=out, begin=begin, count=count):
-                out[count + p] = buf[begin + p]
-                return carry
-
-            lax.fori_loop(0, more, body, 0)
-            count = count + more
-
-
-def early_kernel(meta, recv_list, send_list, slices, buf, total):
+        lax.fori_loop(0, more, body, 0)
+        count = count + more
+
+
+def early_kernel(meta, recv_list, send_list, slices, buf, out, total):
     me = meta[0]
     total[...] = jnp.zeros_like(total)
 
@@ -145,6 +127,7 @@
     for k in range(CS):
         spot = lax.rem(me + NZ - k, NZ) * NQ
         total[spot] = total[spot] + tiles[k]
+    merge(total, out)
 
 
 def merge(total, out):
@@ -166,11 +149,25 @@
     lax.fori_loop(0, NPLANE, body, 0)
 
 
-def late_kernel(near_list, ahead, behind, early, out, total):
-    total[...] = early[...]
-    add_rows(NEAR, near_list, 0, ahead, total)
-    add_rows(NEAR, near_list, NEAR, behind, total)
-    merge(total, out)
+def late_kernel(meta, near_list, near, early, out):
+    out[...] = early[...]
+    side = lax.broadcasted_iota(jnp.int32, (8, 128), 0) // 4
+
+    def body(p, carry):
+        spot = near_list[p]
+        at, q = spot // NQ, spot % NQ
+        h, odd = q // 2, q % 2
+        right = at // NCOL * NCOL + (at + 1) % NCOL
+        tile = near[p]
+        turned = jnp.roll(tile, 4, axis=0)
+        keep = side == odd
+        first = jnp.where(odd == 0, tile, turned)
+        second = jnp.where(odd == 0, turned, tile)
+        out[at, h] = out[at, h] + jnp.where(keep, first, 0.0)
+        out[right, h] = out[right, h] + jnp.where(keep, second, 0.0)
+        return carry
+
+    lax.fori_loop(0, meta[1], body, 0)
 
 
 def full_pack_kernel(send_list, slices, out):
@@ -284,25 +281,20 @@
     origin = (entry >> 4) * SLOTS + ((entry >> 3) & 1) * LIVE + (entry & 7) - CS
     dead = key < 0
     hop = (key - me - line) & 15
-    turn = jnp.where(hop == 0, 15, jnp.where(hop <= AHEAD, hop - 1, 23 - hop))
-    turn = jnp.where(dead, -1, turn)
+    turn = jnp.where(dead, -1, (hop - 1) & 15)
     load = jnp.sum((turn[:, None, :] == step[None, :, None]).astype(jnp.int32), axis=-1)
 
-    inner = (step[:, None] // AHEAD == step[None, :] // AHEAD) & (step[None, :] >= step[:, None])
+    inner = step[None, :] >= step[:, None]
     extra = jnp.where(code == 15, 0, load) - CAP
     run = jnp.sum(jnp.where(inner[None], extra[:, None, :], 0), axis=-1)
     push = run - jnp.minimum(jnp.min(jnp.where(inner[None], run[:, None, :], 0), axis=-1), 0)
     kept = load - push
     place = step[:, None, None]
-    lag = jnp.where(step < AHEAD, -step, step - AHEAD)[None, None, :]
-    meets = ((place + lag - step[None, :, None]) & 15) == 0
-    near = jnp.where(meets, push[None], 0)
-    near_ahead = jnp.sum(jnp.where(code[None] < AHEAD, near, 0), axis=(1, 2))
-    near_behind = jnp.sum(jnp.where(code[None] < AHEAD, 0, near), axis=(1, 2))
+    meets = ((place - step[None, None, :] - step[None, :, None]) & 15) == 0
+    near = jnp.sum(jnp.where(meets, push[None], 0), axis=(1, 2))
     crowded = (
         (jnp.min(kept) < 0)
-        | (jnp.max(near_ahead) > NEAR)
-        | (jnp.max(near_behind) > NEAR)
+        | (jnp.max(near) > NEAR)
         | (jnp.max(push) > LOCAL)
         | (jnp.max(jnp.where(code == 15, load, 0)) > LOCAL)
     )
@@ -311,11 +303,9 @@
     sent = turn[0][None] == step[:, None]
     rank = ranks_of(jnp.concatenate([mine, sent], axis=0), before)
     rank_mine, rank_sent = rank[:NZ], rank[NZ:]
-    own_code = jnp.where(line == 0, 15, jnp.where(line < 8, 7 + line, 15 - line))
-    push_mine = jnp.sum(jnp.where(code == own_code, push, 0), axis=1)
+    push_mine = jnp.sum(jnp.where(code == 15 - line, push, 0), axis=1)
     spots_mine = jnp.where(mine, rank_mine - push_mine[:, None], -1)
-    sooner = (line // 8 == code // 8) & jnp.where(line < 8, code < line, code > line)
-    base = jnp.sum(jnp.where(sooner, push_mine[None], 0), axis=1)
+    base = jnp.sum(jnp.where(code > line, push_mine[None], 0), axis=1)
     spots_near = jnp.where(
         mine & (rank_mine < push_mine[:, None]), base[:, None] + rank_mine, -1
     )
@@ -323,26 +313,23 @@
     stay = jnp.where(sent & (rank_sent >= push_own), rank_sent - push_own, -1)
     moved = jnp.where(sent & (rank_sent < push_own), rank_sent, -1)
     above = jnp.concatenate([moved[1:], moved[:1]], axis=0)
-    rides = (above >= 0) & (line != FARTHEST) & (line < 14)
+    rides = (above >= 0) & (line < 14)
     spots_sent = jnp.where(rides, kept[0][:, None] + above, stay)
     table = lists_of(
-        jnp.concatenate([spots_mine, spots_sent, moved[:1], moved[8:9]], axis=0),
-        jnp.concatenate([spot, jnp.broadcast_to(origin[None], (NZ + 2, NPLANE * 16))], axis=0),
+        jnp.concatenate([spots_mine, spots_sent, moved[:1]], axis=0),
+        jnp.concatenate([spot, jnp.broadcast_to(origin[None], (NZ + 1, NPLANE * 16))], axis=0),
         LOCAL,
     )
     recv_list = (table[:NZ] + TRASH).reshape(-1)
     send_list = table[NZ:].reshape(-1)
     at = jnp.arange(NEAR, dtype=jnp.int32)[:, None, None]
     near_hits = jnp.where(spots_near[None] == at, spot[None], 0)
-    near_list = (
-        jnp.stack([jnp.sum(near_hits[:, 8:], axis=(1, 2)), jnp.sum(near_hits[:, :8], axis=(1, 2))])
-        + TRASH
-    ).reshape(-1)
+    near_list = jnp.sum(near_hits, axis=(1, 2)) + TRASH
+    meta = jnp.stack([me, jnp.sum(push_mine)])
     push_flat, kept_flat = push.reshape(-1), kept.reshape(-1)
-    recv_list, send_list, near_list, push_flat, kept_flat, crowded = lax.optimization_barrier(
-        (recv_list, send_list, near_list, push_flat, kept_flat, crowded)
-    )
-    meta = me.reshape(1)
+    meta, recv_list, send_list, near_list, push_flat, kept_flat, crowded = lax.optimization_barrier(
+        (meta, recv_list, send_list, near_list, push_flat, kept_flat, crowded)
+    )
 
     def fast(spread):
         buf = kernel_call(
@@ -352,27 +339,26 @@
             out_specs=VMEM,
         )(meta, send_list, spread)
         buf = lax.all_to_all(buf, "z", 0, 0, tiled=True)
-        ahead, behind = kernel_call(
+        near = kernel_call(
             relay_kernel,
-            out_shape=[shape_of(NEAR, 8, 128)] * 2,
+            out_shape=shape_of(NEAR, 8, 128),
             in_specs=[SMEM] * 4 + [VMEM] * 2,
-            out_specs=[VMEM] * 2,
+            out_specs=VMEM,
         )(meta, push_flat, kept_flat, send_list, spread, buf)
-        ahead = lax.ppermute(ahead, "z", [(i, (i + 1) % NZ) for i in range(NZ)])
-        behind = lax.ppermute(behind, "z", [(i, (i - 1) % NZ) for i in range(NZ)])
-        total = kernel_call(
+        near = lax.ppermute(near, "z", [(i, (i + 1) % NZ) for i in range(NZ)])
+        early = kernel_call(
             early_kernel,
-            out_shape=shape_of(TRASH + 1, 8, 128),
+            out_shape=MERGED,
             in_specs=[SMEM] * 3 + [VMEM] * 2,
             out_specs=VMEM,
+            scratch_shapes=[TOTAL],
         )(meta, recv_list, send_list, spread, buf)
         return kernel_call(
             late_kernel,
             out_shape=MERGED,
-            in_specs=[SMEM] + [VMEM] * 3,
-            out_specs=VMEM,
-            scratch_shapes=[TOTAL],
-        )(near_list, ahead, behind, total)
+            in_specs=[SMEM] * 2 + [VMEM] * 2,
+            out_specs=VMEM,
+        )(meta, near_list, near, early)
 
     def full(spread):
         plane = jnp.where(dead, NZ, key & 15)

time: 174 us -> 172 us (0.989)
  starting transfers between devices: 20.1 us -> 15.6 us
  waiting for transfers between devices: 13 us -> 17.4 us
    ppermute x2 -> x1, starting transfers between devices: 9.43 us -> 4.94 us  [fast(): near = lax.ppermute(near, 'z', [(i, (i + 1) % NZ) for i in range(NZ)])]
    ppermute x2 -> x1, waiting for transfers between devices: 0.01 us -> 2.77 us  [fast(): near = lax.ppermute(near, 'z', [(i, (i + 1) % NZ) for i in range(NZ)])]
  transfers between devices with their start and end apart: 3 -> 2, of which waited for: 1 -> 2; matrix products, arithmetic and copies ran while one was open for 5% -> 5% of each run, Pallas kernels for 2% -> 2%
where the time goes in v4:
time: 172 us
  blocking collectives  114 us (66%)
  waiting for transfers between devices  17.4 us (10%)
  starting transfers between devices  15.6 us (9%)
  Pallas kernels  9.7 us (6%)
  other arithmetic  7.48 us (4%)
  matrix products  4.01 us (2%)
  between operations  3.01 us (2%)
    all_to_all x1, blocking collectives, fast(): buf = lax.all_to_all(buf, 'z', 0, 0, tiled=True)  80.4 us
    all_to_all x1, blocking collectives, on_device(): parts = lax.all_to_all(merged, PLANE, 0, 0, tiled=True)  33.6 us
    all_to_all x1, waiting for transfers between devices, on_device(): lax.all_to_all(slices, PLANE, 0, 0, tiled=True)  14.6 us
    all_to_all x1, starting transfers between devices, on_device(): lax.all_to_all(slices, PLANE, 0, 0, tiled=True)  10.7 us
    ppermute x1, starting transfers between devices, fast(): near = lax.ppermute(near, 'z', [(i, (i + 1) % NZ) for i in range(NZ)])  4.94 us
    pallas_call x1, Pallas kernels, fast(): kernel_call(early_kernel, out_shape=MERGED, in_specs=[SMEM] * 3 + [VMEM]...  3.5 us
  transfers between devices with their start and end apart: 2, of which 2 were waited for; matrix products, arithmetic and copies ran while one was open for 5% of the time, Pallas kernels for 2%

profile of v4, /device:TPU:1, one launch (start us, length us, event | category | flops | bytes accessed | tf_op | source)
XLA Modules:
  0.0 172.1 jit_solution(13421595147991294200)
XLA Ops:
  0.0 2.2 %convolution_convert_fusion.1 = bf16[472,1024]{1,0:T(8,128)(2,1)S(1)} fusion(bf16[944,1024]{1,0:T(8,128)(2,1)} %param.10, bf16[944,472]{1,0:T(8,128)(2,1)} %param.9), kind=kOutput, calls=%fused_computation.21 | convolution fusion | flops 456744960 | bytes 2416640 | tf_op jit(solution)/shard_map/dot_general | solution.py:252
  2.2 0.7 convolution_convert_fusion.2
  2.9 0.5 fusion.12.second
  3.4 0.5 fusion.14.first
  3.9 1.4 shard_map.55
  5.3 10.7 %all-to-all-start.2 = ((f32[32,14,8,128]{3,2,1,0:T(8,128)}), f32[32,14,8,128]{3,2,1,0:T(8,128)S(1)}, u32[]{:S(2)}, u32[]{:S(2)}) async-start(f32[32,14,8,128]{3,2,1,0:T(8,128)} %shard_map.55), calls=%async_computation.2 | async-start | bytes 3670016 | tf_op jit(solution)/shard_map/all_to_all | solution.py:269
  16.1 0.2 copy.10
  16.3 0.3 reshape.138
  16.7 0.4 convert_reduce_fusion
  17.2 0.7 select_reduce_fusion.6
  17.9 0.3 select_reduce_fusion.5
  18.2 0.3 select_reduce_fusion.4
  18.6 0.7 fusion.34
  19.4 0.8 fusion.24
  20.2 0.1 select_reduce_fusion.7
  20.3 0.2 convolution_convert_fusion.3
  22.7 0.7 select_reduce_fusion.1
  23.6 0.4 select_reduce_fusion.3
  24.0 0.7 reduce_max.27
  25.4 0.6 pad_add_fusion.4
  26.1 1.3 select_reduce_fusion.2
  27.4 14.6 %all-to-all-done.2 = f32[32,14,8,128]{3,2,1,0:T(8,128)S(1)} async-done(((f32[32,14,8,128]{3,2,1,0:T(8,128)}), f32[32,14,8,128]{3,2,1,0:T(8,128)S(1)}, u32[]{:S(2)}, u32[]{:S(2)}) %all-to-all-start.2) | async-done | bytes 1835040 | tf_op jit(solution)/shard_map/all_to_all | solution.py:269
  42.0 95.0 %conditional.1 = (f32[32,12,8,128]{3,2,1,0:T(8,128)S(1)}) conditional(s32[]{:T(128)} %convert_element_type.25, (s32[2]{0:T(128)S(1)}, s32[680]{0:T(1024)S(1)}, f32[448,8,128]{2,1,0:T(8,128)S(1)}, s32[256]{0:T(256)S(1)}, s32[256]{0:T(256)S(1)}, /*index=5*/s32[640]{0:T(1024)S(1)}, s32[64]{0:T(128)S(1)}) %tuple.28, (s32[16,512]{1,0:T(8,128)S(1)}, ...), branch_computations={%region_13.14_spmd, %region_14.16_spmd} | conditional | flops 20018704 | bytes 31249188 | solution.py:386
  42.0 0.9 branch_0_fun.4
  43.0 80.4 %all_to_all.18.buf = f32[384,8,128]{2,1,0:T(8,128)S(1)} all-to-all(f32[384,8,128]{2,1,0:T(8,128)S(1)} %branch_0_fun.4), channel_id=1, replica_groups=mesh['ylo'=2,'z'=16,'x'=4,'yhi'=2,'core'=2] {'z'}, dimensions={0} | all-to-all | bytes 3145728 | tf_op jit(solution)/shard_map/cond/branch_0_fun/all_to_all | solution.py:341
  123.4 0.9 branch_0_fun.5
  124.3 4.9 %collective-permute-start = (f32[64,8,128]{2,1,0:T(8,128)S(1)}, f32[64,8,128]{2,1,0:T(8,128)S(1)}, u32[]{:S(2)}, u32[]{:S(2)}) collective-permute-start(f32[64,8,128]{2,1,0:T(8,128)S(1)} %branch_0_fun.5), channel_id=1, source_target_pairs={{0,16},{16,32},{32,48},{48,64},{64,80},{80,96},{96,112},{112,128},... | collective-permute-start | bytes 786440 | tf_op jit(solution)/shard_map/cond/branch_0_fun/ppermute | solution.py:348
  129.3 3.5 %branch_0_fun.6.early = f32[32,12,8,128]{3,2,1,0:T(8,128)S(1)} custom-call(s32[2]{0:T(128)S(1)} %get-tuple-element.67.meta, s32[640]{0:T(1024)S(1)} %get-tuple-element.73.recv_list, s32[680]{0:T(1024)S(1)} %get-tuple-element.71.send_list, f32[448,8,128]{2,1,0:T(8,128)S(1)} %get-tuple-element.72.slices, f32[384,8,128]{2,1,0:T(8,128)S(1)} %all_to_all.18.buf), custom_call_target="tpu_custom_call" | custom-call | tf_op jit(solution)/shard_map/cond/branch_0_fun/pallas_call | solution.py:349
  132.8 2.8 %collective-permute-done.near = f32[64,8,128]{2,1,0:T(8,128)S(1)} collective-permute-done((f32[64,8,128]{2,1,0:T(8,128)S(1)}, f32[64,8,128]{2,1,0:T(8,128)S(1)}, u32[]{:S(2)}, u32[]{:S(2)}) %collective-permute-start) | collective-permute-done | bytes 262176 | tf_op jit(solution)/shard_map/cond/branch_0_fun/ppermute | solution.py:348
  135.5 1.5 branch_0_fun.7
  137.0 33.6 %all_to_all.19.parts = f32[32,12,8,128]{3,2,1,0:T(8,128)S(1)} all-to-all(f32[32,12,8,128]{3,2,1,0:T(8,128)S(1)} %get-tuple-element.117), channel_id=1, replica_groups=mesh['ylo'=2,'z'=16,'x'=4,'yhi'=2,'core'=2] {'ylo','x','yhi','core'}, dimensions={0} | all-to-all | bytes 3145728 | tf_op jit(solution)/shard_map/all_to_all | solution.py:387
  170.6 1.5 shard_map.56
  (44 shorter events, 0.8 us)
Async XLA Ops:
  0.0 2.2 %copy-start.4 = (bf16[944,1024]{1,0:T(8,128)(2,1)S(1)}, bf16[944,1024]{1,0:T(8,128)(2,1)}, u32[]{:S(2)}) copy-start(bf16[944,1024]{1,0:T(8,128)(2,1)} %param.10) | copy-start | bytes 5799940
  0.0 2.2 %copy-start.5 = (bf16[944,472]{1,0:T(8,128)(2,1)S(1)}, bf16[944,472]{1,0:T(8,128)(2,1)}, u32[]{:S(2)}) copy-start(bf16[944,472]{1,0:T(8,128)(2,1)} %param.9) | copy-start | bytes 2673412
  5.3 10.7 %copy-start.2 = (s32[1024,8]{0,1:T(8,128)S(1)}, s32[1024,8]{0,1:T(8,128)}, u32[]{:S(2)}) copy-start(s32[1024,8]{0,1:T(8,128)} %param.7) | copy-start | bytes 98308
  5.3 10.8 %copy-start.3 = (s32[1024]{0:T(1024)S(1)}, s32[1024]{0:T(1024)}, u32[]{:S(2)}) copy-start(s32[1024]{0:T(1024)} %param.8) | copy-start | bytes 12292
  5.3 36.7 %all-to-all-start.2 = ((f32[32,14,8,128]{3,2,1,0:T(8,128)}), f32[32,14,8,128]{3,2,1,0:T(8,128)S(1)}, u32[]{:S(2)}, u32[]{:S(2)}) async-start(f32[32,14,8,128]{3,2,1,0:T(8,128)} %shard_map.55), calls=%async_computation.2 | async-start | bytes 3670016 | tf_op jit(solution)/shard_map/all_to_all | solution.py:269
  124.3 11.2 %collective-permute-start = (f32[64,8,128]{2,1,0:T(8,128)S(1)}, f32[64,8,128]{2,1,0:T(8,128)S(1)}, u32[]{:S(2)}, u32[]{:S(2)}) collective-permute-start(f32[64,8,128]{2,1,0:T(8,128)S(1)} %branch_0_fun.5), channel_id=1, source_target_pairs={{0,16},{16,32},{32,48},{48,64},{64,80},{80,96},{96,112},{112,128},... | collective-permute-start | bytes 786440 | tf_op jit(solution)/shard_map/cond/branch_0_fun/ppermute | solution.py:348
  137.0 33.6 %copy-start.1 = (bf16[24,128,1,128]{3,1,2,0:T(8,128)(2,1)S(1)}, bf16[24,128,1,128]{3,1,2,0:T(8,128)(2,1)}, u32[]{:S(2)}) copy-start(bf16[24,128,1,128]{3,1,2,0:T(8,128)(2,1)} %param.11) | copy-start | bytes 2359300

commit v5 on v4

--- a/solution.py
+++ b/solution.py
@@ -10,7 +10,7 @@
 CS = 2
 YLO, NZ, XS, YHI, CORE = 2, 16, 4, 2, 2
 NCOL = XS * YHI * CORE
-PLANE = ("ylo", "x", "yhi", "core")
+PLANE = ("x", "yhi", "ylo", "core")
 NPLANE = YLO * NCOL
 LIVE = 6
 SLOTS = 2 * LIVE + CS
@@ -58,11 +58,15 @@
         )
 
 
+def place_of(ylo, col):
+    return col // CORE * (YLO * CORE) + ylo * CORE + col % CORE
+
+
 def shared_slice(slices, target, k):
     source = lax.rem(target + NZ - k, NZ)
     return (
-        slices[source * SLOTS + 2 * LIVE + k]
-        + slices[(NCOL + source) * SLOTS + 2 * LIVE + k]
+        slices[place_of(0, source) * SLOTS + 2 * LIVE + k]
+        + slices[place_of(1, source) * SLOTS + 2 * LIVE + k]
     )
 
 
@@ -136,12 +140,13 @@
     def body(at, carry):
         side = at // NCOL * NCOL
         left = lax.rem(at + NCOL - 1, NCOL) + side
+        place = place_of(at // NCOL, at % NCOL)
         for h in range(NQ // 2):
             a0 = total[at * NQ + 2 * h]
             a1 = total[at * NQ + 2 * h + 1]
             b0 = total[left * NQ + 2 * h]
             b1 = total[left * NQ + 2 * h + 1]
-            out[at, h] = jnp.where(
+            out[place, h] = jnp.where(
                 low, a0 + jnp.roll(b0, 4, axis=0), jnp.roll(a1, 4, axis=0) + b1
             )
         return carry
@@ -157,13 +162,14 @@
         spot = near_list[p]
         at, q = spot // NQ, spot % NQ
         h, odd = q // 2, q % 2
-        right = at // NCOL * NCOL + (at + 1) % NCOL
+        here = place_of(at // NCOL, at % NCOL)
+        right = place_of(at // NCOL, (at + 1) % NCOL)
         tile = near[p]
         turned = jnp.roll(tile, 4, axis=0)
         keep = side == odd
         first = jnp.where(odd == 0, tile, turned)
         second = jnp.where(odd == 0, turned, tile)
-        out[at, h] = out[at, h] + jnp.where(keep, first, 0.0)
+        out[here, h] = out[here, h] + jnp.where(keep, first, 0.0)
         out[right, h] = out[right, h] + jnp.where(keep, second, 0.0)
         return carry
 
@@ -278,7 +284,7 @@
     step = jnp.arange(NZ, dtype=jnp.int32)
     line, code = step[:, None], step[None, :]
     spot = (((key >> 4) & 1) * NCOL + ((entry >> 4) & 15)[None]) * NQ + (key >> 5) - TRASH
-    origin = (entry >> 4) * SLOTS + ((entry >> 3) & 1) * LIVE + (entry & 7) - CS
+    origin = place_of(entry >> 8, (entry >> 4) & 15) * SLOTS + ((entry >> 3) & 1) * LIVE + (entry & 7) - CS
     dead = key < 0
     hop = (key - me - line) & 15
     turn = jnp.where(dead, -1, (hop - 1) & 15)

time: 172 us -> 172 us (level)
  no operation moved by 1% of the time
where the time goes in v5:
time: 172 us; the launch traced here: 171 us
  blocking collectives  113 us (66%)
  waiting for transfers between devices  16.7 us (10%)
  starting transfers between devices  15.5 us (9%)
  Pallas kernels  10.3 us (6%)
  other arithmetic  7.52 us (4%)
  matrix products  4.01 us (2%)
  between operations  3.04 us (2%)
    all_to_all x1, blocking collectives, fast(): buf = lax.all_to_all(buf, 'z', 0, 0, tiled=True)  80.6 us
    all_to_all x1, blocking collectives, on_device(): parts = lax.all_to_all(merged, PLANE, 0, 0, tiled=True)  32.7 us
    all_to_all x1, waiting for transfers between devices, on_device(): lax.all_to_all(slices, PLANE, 0, 0, tiled=True)  14.1 us
    all_to_all x1, starting transfers between devices, on_device(): lax.all_to_all(slices, PLANE, 0, 0, tiled=True)  10.7 us
    ppermute x1, starting transfers between devices, fast(): near = lax.ppermute(near, 'z', [(i, (i + 1) % NZ) for i in range(NZ)])  4.81 us
    pallas_call x1, Pallas kernels, fast(): kernel_call(early_kernel, out_shape=MERGED, in_specs=[SMEM] * 3 + [VMEM]...  3.66 us
  transfers between devices with their start and end apart: 2, of which 2 were waited for; matrix products, arithmetic and copies ran while one was open for 5% of the time, Pallas kernels for 2%

profile of v5, /device:TPU:1, one launch (start us, length us, event | category | flops | bytes accessed | tf_op | source)
XLA Modules:
  0.0 171.2 jit_solution(4833523533446359877)
XLA Ops:
  0.0 2.2 %convolution_convert_fusion.1 = bf16[472,1024]{1,0:T(8,128)(2,1)S(1)} fusion(bf16[944,1024]{1,0:T(8,128)(2,1)} %param.10, bf16[944,472]{1,0:T(8,128)(2,1)} %param.9), kind=kOutput, calls=%fused_computation.33 | convolution fusion | flops 456744960 | bytes 2416640 | tf_op jit(solution)/shard_map/dot_general | solution.py:258
  2.2 0.7 convolution_convert_fusion.2
  2.9 0.5 fusion.21.second
  3.4 0.5 fusion.23.first
  3.9 1.4 shard_map.55
  5.3 10.7 %all-to-all-start.2 = ((f32[32,14,8,128]{3,2,1,0:T(8,128)}), f32[32,14,8,128]{3,2,1,0:T(8,128)S(1)}, u32[]{:S(2)}, u32[]{:S(2)}) async-start(f32[32,14,8,128]{3,2,1,0:T(8,128)} %shard_map.55), calls=%async_computation.2 | async-start | bytes 3670016 | tf_op jit(solution)/shard_map/all_to_all | solution.py:275
  16.1 0.2 copy.10
  16.3 0.3 reshape.170
  16.7 0.4 convert_reduce_fusion
  17.2 0.7 select_reduce_fusion.6
  17.9 0.3 select_reduce_fusion.5
  18.2 0.3 select_reduce_fusion.4
  18.6 0.7 fusion.50
  19.4 0.8 fusion.33
  20.2 0.1 select_reduce_fusion.7
  20.3 0.2 convolution_convert_fusion.3
  22.8 0.7 select_reduce_fusion.1
  23.6 0.4 select_reduce_fusion.3
  24.0 0.7 reduce_max.27
  25.4 0.6 pad_add_fusion.4
  26.1 1.3 select_reduce_fusion.2
  27.4 14.1 %all-to-all-done.2 = f32[32,14,8,128]{3,2,1,0:T(8,128)S(1)} async-done(((f32[32,14,8,128]{3,2,1,0:T(8,128)}), f32[32,14,8,128]{3,2,1,0:T(8,128)S(1)}, u32[]{:S(2)}, u32[]{:S(2)}) %all-to-all-start.2) | async-done | bytes 1835040 | tf_op jit(solution)/shard_map/all_to_all | solution.py:275
  41.5 95.4 %conditional.1 = (f32[32,12,8,128]{3,2,1,0:T(8,128)S(1)}) conditional(s32[]{:T(128)} %convert_element_type.25, (s32[2]{0:T(128)S(1)}, s32[680]{0:T(1024)S(1)}, f32[448,8,128]{2,1,0:T(8,128)S(1)}, s32[256]{0:T(256)S(1)}, s32[256]{0:T(256)S(1)}, /*index=5*/s32[640]{0:T(1024)S(1)}, s32[64]{0:T(128)S(1)}) %tuple.29, (s32[16,512]{1,0:T(8,128)S(1)}, ...), branch_computations={%region_13.14_spmd, %region_14.16_spmd} | conditional | flops 20027408 | bytes 31266084 | solution.py:392
  41.6 1.1 branch_0_fun.4
  42.7 80.6 %all_to_all.18.buf = f32[384,8,128]{2,1,0:T(8,128)S(1)} all-to-all(f32[384,8,128]{2,1,0:T(8,128)S(1)} %branch_0_fun.4), channel_id=1, replica_groups=mesh['ylo'=2,'z'=16,'x'=4,'yhi'=2,'core'=2] {'z'}, dimensions={0} | all-to-all | bytes 3145728 | tf_op jit(solution)/shard_map/cond/branch_0_fun/all_to_all | solution.py:347
  123.3 0.9 branch_0_fun.5
  124.1 4.8 %collective-permute-start = (f32[64,8,128]{2,1,0:T(8,128)S(1)}, f32[64,8,128]{2,1,0:T(8,128)S(1)}, u32[]{:S(2)}, u32[]{:S(2)}) collective-permute-start(f32[64,8,128]{2,1,0:T(8,128)S(1)} %branch_0_fun.5), channel_id=1, source_target_pairs={{0,16},{16,32},{32,48},{48,64},{64,80},{80,96},{96,112},{112,128},... | collective-permute-start | bytes 786440 | tf_op jit(solution)/shard_map/cond/branch_0_fun/ppermute | solution.py:354
  129.0 3.7 %branch_0_fun.6.early = f32[32,12,8,128]{3,2,1,0:T(8,128)S(1)} custom-call(s32[2]{0:T(128)S(1)} %get-tuple-element.111.meta, s32[640]{0:T(1024)S(1)} %get-tuple-element.117.recv_list, s32[680]{0:T(1024)S(1)} %get-tuple-element.115.send_list, f32[448,8,128]{2,1,0:T(8,128)S(1)} %get-tuple-element.116.slices, f32[384,8,128]{2,1,0:T(8,128)S(1)} %all_to_all.18.buf), custom_call_target="tpu_custom_call" | custom-call | tf_op jit(solution)/shard_map/cond/branch_0_fun/pallas_call | solution.py:355
  132.6 2.6 %collective-permute-done.near = f32[64,8,128]{2,1,0:T(8,128)S(1)} collective-permute-done((f32[64,8,128]{2,1,0:T(8,128)S(1)}, f32[64,8,128]{2,1,0:T(8,128)S(1)}, u32[]{:S(2)}, u32[]{:S(2)}) %collective-permute-start) | collective-permute-done | bytes 262176 | tf_op jit(solution)/shard_map/cond/branch_0_fun/ppermute | solution.py:354
  135.2 1.7 %branch_0_fun.7 = f32[32,12,8,128]{3,2,1,0:T(8,128)S(1)} custom-call(s32[2]{0:T(128)S(1)} %get-tuple-element.111.meta, s32[64]{0:T(128)S(1)} %get-tuple-element.112.near_list, f32[64,8,128]{2,1,0:T(8,128)S(1)} %collective-permute-done.near, f32[32,12,8,128]{3,2,1,0:T(8,128)S(1)} %branch_0_fun.6.early), custom_call_target="tpu_custom_call" | custom-call | tf_op jit(solution)/shard_map/cond/branch_0_fun/pallas_call | solution.py:362
  137.0 32.7 %all_to_all.19.parts = f32[32,12,8,128]{3,2,1,0:T(8,128)S(1)} all-to-all(f32[32,12,8,128]{3,2,1,0:T(8,128)S(1)} %get-tuple-element.172), channel_id=1, replica_groups=mesh['ylo'=2,'z'=16,'x'=4,'yhi'=2,'core'=2] {'x','yhi','ylo','core'}, dimensions={0} | all-to-all | bytes 3145728 | tf_op jit(solution)/shard_map/all_to_all | solution.py:393
  169.7 1.5 shard_map.56
  (51 shorter events, 0.9 us)
Async XLA Ops:
  0.0 2.2 %copy-start.4 = (bf16[944,1024]{1,0:T(8,128)(2,1)S(1)}, bf16[944,1024]{1,0:T(8,128)(2,1)}, u32[]{:S(2)}) copy-start(bf16[944,1024]{1,0:T(8,128)(2,1)} %param.10) | copy-start | bytes 5799940
  0.0 2.2 %copy-start.5 = (bf16[944,472]{1,0:T(8,128)(2,1)S(1)}, bf16[944,472]{1,0:T(8,128)(2,1)}, u32[]{:S(2)}) copy-start(bf16[944,472]{1,0:T(8,128)(2,1)} %param.9) | copy-start | bytes 2673412
  5.3 10.8 %copy-start.2 = (s32[1024,8]{0,1:T(8,128)S(1)}, s32[1024,8]{0,1:T(8,128)}, u32[]{:S(2)}) copy-start(s32[1024,8]{0,1:T(8,128)} %param.7) | copy-start | bytes 98308
  5.3 10.8 %copy-start.3 = (s32[1024]{0:T(1024)S(1)}, s32[1024]{0:T(1024)}, u32[]{:S(2)}) copy-start(s32[1024]{0:T(1024)} %param.8) | copy-start | bytes 12292
  5.3 36.2 %all-to-all-start.2 = ((f32[32,14,8,128]{3,2,1,0:T(8,128)}), f32[32,14,8,128]{3,2,1,0:T(8,128)S(1)}, u32[]{:S(2)}, u32[]{:S(2)}) async-start(f32[32,14,8,128]{3,2,1,0:T(8,128)} %shard_map.55), calls=%async_computation.2 | async-start | bytes 3670016 | tf_op jit(solution)/shard_map/all_to_all | solution.py:275
  124.1 11.1 %collective-permute-start = (f32[64,8,128]{2,1,0:T(8,128)S(1)}, f32[64,8,128]{2,1,0:T(8,128)S(1)}, u32[]{:S(2)}, u32[]{:S(2)}) collective-permute-start(f32[64,8,128]{2,1,0:T(8,128)S(1)} %branch_0_fun.5), channel_id=1, source_target_pairs={{0,16},{16,32},{32,48},{48,64},{64,80},{80,96},{96,112},{112,128},... | collective-permute-start | bytes 786440 | tf_op jit(solution)/shard_map/cond/branch_0_fun/ppermute | solution.py:354
  137.0 32.7 %copy-start.1 = (bf16[24,128,1,128]{3,1,2,0:T(8,128)(2,1)S(1)}, bf16[24,128,1,128]{3,1,2,0:T(8,128)(2,1)}, u32[]{:S(2)}) copy-start(bf16[24,128,1,128]{3,1,2,0:T(8,128)(2,1)} %param.11) | copy-start | bytes 2359300

commit v6 on v5

--- a/solution.py
+++ b/solution.py
@@ -16,7 +16,7 @@
 SLOTS = 2 * LIVE + CS
 NQ = 24
 CAP = 22
-NEAR = 64
+NEAR = 56
 LOCAL = 40
 FULL = 64
 TRASH = NPLANE * NQ

time: 172 us -> 171 us (level)
  no operation moved by 1% of the time
where the time goes in v6:
time: 171 us
  blocking collectives  113 us (66%)
  waiting for transfers between devices  16.5 us (10%)
  starting transfers between devices  15.5 us (9%)
  Pallas kernels  10.2 us (6%)
  other arithmetic  7.37 us (4%)
  matrix products  4.01 us (2%)
  between operations  3.04 us (2%)
    all_to_all x1, blocking collectives, fast(): buf = lax.all_to_all(buf, 'z', 0, 0, tiled=True)  80.6 us
    all_to_all x1, blocking collectives, on_device(): parts = lax.all_to_all(merged, PLANE, 0, 0, tiled=True)  32.7 us
    all_to_all x1, waiting for transfers between devices, on_device(): lax.all_to_all(slices, PLANE, 0, 0, tiled=True)  14.2 us
    all_to_all x1, starting transfers between devices, on_device(): lax.all_to_all(slices, PLANE, 0, 0, tiled=True)  10.7 us
    ppermute x1, starting transfers between devices, fast(): near = lax.ppermute(near, 'z', [(i, (i + 1) % NZ) for i in range(NZ)])  4.87 us
    pallas_call x1, Pallas kernels, fast(): kernel_call(early_kernel, out_shape=MERGED, in_specs=[SMEM] * 3 + [VMEM]...  3.66 us
  transfers between devices with their start and end apart: 2, of which 2 were waited for; matrix products, arithmetic and copies ran while one was open for 5% of the time, Pallas kernels for 2%

profile of v6, /device:TPU:1, one launch (start us, length us, event | category | flops | bytes accessed | tf_op | source)
XLA Modules:
  0.0 170.8 jit_solution(7869127004834696784)
XLA Ops:
  0.0 2.2 %convolution_convert_fusion.1 = bf16[472,1024]{1,0:T(8,128)(2,1)S(1)} fusion(bf16[944,1024]{1,0:T(8,128)(2,1)} %param.10, bf16[944,472]{1,0:T(8,128)(2,1)} %param.9), kind=kOutput, calls=%fused_computation.33 | convolution fusion | flops 456744960 | bytes 2416640 | tf_op jit(solution)/shard_map/dot_general | solution.py:258
  2.2 0.7 convolution_convert_fusion.2
  2.9 0.5 fusion.21.second
  3.4 0.5 fusion.23.first
  3.9 1.4 shard_map.55
  5.3 10.7 %all-to-all-start.2 = ((f32[32,14,8,128]{3,2,1,0:T(8,128)}), f32[32,14,8,128]{3,2,1,0:T(8,128)S(1)}, u32[]{:S(2)}, u32[]{:S(2)}) async-start(f32[32,14,8,128]{3,2,1,0:T(8,128)} %shard_map.55), calls=%async_computation.2 | async-start | bytes 3670016 | tf_op jit(solution)/shard_map/all_to_all | solution.py:275
  16.1 0.2 copy.10
  16.3 0.3 reshape.170
  16.7 0.4 convert_reduce_fusion
  17.2 0.7 select_reduce_fusion.6
  17.9 0.3 select_reduce_fusion.5
  18.2 0.3 select_reduce_fusion.4
  18.6 0.7 fusion.50
  19.4 0.8 fusion.33
  20.2 0.1 select_reduce_fusion.7
  20.3 0.2 convolution_convert_fusion.3
  22.8 0.7 select_reduce_fusion.1
  23.6 0.4 select_reduce_fusion.3
  24.0 0.7 reduce_max.27
  25.4 0.6 pad_add_fusion.4
  26.1 1.1 select_reduce_fusion.2
  27.3 14.2 %all-to-all-done.2 = f32[32,14,8,128]{3,2,1,0:T(8,128)S(1)} async-done(((f32[32,14,8,128]{3,2,1,0:T(8,128)}), f32[32,14,8,128]{3,2,1,0:T(8,128)S(1)}, u32[]{:S(2)}, u32[]{:S(2)}) %all-to-all-start.2) | async-done | bytes 1835040 | tf_op jit(solution)/shard_map/all_to_all | solution.py:275
  41.5 95.1 %conditional.1 = (f32[32,12,8,128]{3,2,1,0:T(8,128)S(1)}) conditional(s32[]{:T(128)} %convert_element_type.25, (s32[2]{0:T(128)S(1)}, s32[680]{0:T(1024)S(1)}, f32[448,8,128]{2,1,0:T(8,128)S(1)}, s32[256]{0:T(256)S(1)}, s32[256]{0:T(256)S(1)}, /*index=5*/s32[640]{0:T(1024)S(1)}, s32[56]{0:T(128)S(1)}) %tuple.29, (s32[16,512]{1,0:T(8,128)S(1)}, ...), branch_computations={%region_13.14_spmd, %region_14.16_spmd} | conditional | flops 20027408 | bytes 31266084 | solution.py:392
  41.6 1.1 branch_0_fun.4
  42.7 80.6 %all_to_all.18.buf = f32[384,8,128]{2,1,0:T(8,128)S(1)} all-to-all(f32[384,8,128]{2,1,0:T(8,128)S(1)} %branch_0_fun.4), channel_id=1, replica_groups=mesh['ylo'=2,'z'=16,'x'=4,'yhi'=2,'core'=2] {'z'}, dimensions={0} | all-to-all | bytes 3145728 | tf_op jit(solution)/shard_map/cond/branch_0_fun/all_to_all | solution.py:347
  123.3 0.8 branch_0_fun.5
  124.1 4.9 %collective-permute-start = (f32[56,8,128]{2,1,0:T(8,128)S(1)}, f32[56,8,128]{2,1,0:T(8,128)S(1)}, u32[]{:S(2)}, u32[]{:S(2)}) collective-permute-start(f32[56,8,128]{2,1,0:T(8,128)S(1)} %branch_0_fun.5), channel_id=1, source_target_pairs={{0,16},{16,32},{32,48},{48,64},{64,80},{80,96},{96,112},{112,128},... | collective-permute-start | bytes 688136 | tf_op jit(solution)/shard_map/cond/branch_0_fun/ppermute | solution.py:354
  128.9 3.7 %branch_0_fun.6.early = f32[32,12,8,128]{3,2,1,0:T(8,128)S(1)} custom-call(s32[2]{0:T(128)S(1)} %get-tuple-element.111.meta, s32[640]{0:T(1024)S(1)} %get-tuple-element.117.recv_list, s32[680]{0:T(1024)S(1)} %get-tuple-element.115.send_list, f32[448,8,128]{2,1,0:T(8,128)S(1)} %get-tuple-element.116.slices, f32[384,8,128]{2,1,0:T(8,128)S(1)} %all_to_all.18.buf), custom_call_target="tpu_custom_call" | custom-call | tf_op jit(solution)/shard_map/cond/branch_0_fun/pallas_call | solution.py:355
  132.6 2.3 %collective-permute-done.near = f32[56,8,128]{2,1,0:T(8,128)S(1)} collective-permute-done((f32[56,8,128]{2,1,0:T(8,128)S(1)}, f32[56,8,128]{2,1,0:T(8,128)S(1)}, u32[]{:S(2)}, u32[]{:S(2)}) %collective-permute-start) | collective-permute-done | bytes 229408 | tf_op jit(solution)/shard_map/cond/branch_0_fun/ppermute | solution.py:354
  134.9 1.7 %branch_0_fun.7 = f32[32,12,8,128]{3,2,1,0:T(8,128)S(1)} custom-call(s32[2]{0:T(128)S(1)} %get-tuple-element.111.meta, s32[56]{0:T(128)S(1)} %get-tuple-element.112.near_list, f32[56,8,128]{2,1,0:T(8,128)S(1)} %collective-permute-done.near, f32[32,12,8,128]{3,2,1,0:T(8,128)S(1)} %branch_0_fun.6.early), custom_call_target="tpu_custom_call" | custom-call | tf_op jit(solution)/shard_map/cond/branch_0_fun/pallas_call | solution.py:362
  136.7 32.7 %all_to_all.19.parts = f32[32,12,8,128]{3,2,1,0:T(8,128)S(1)} all-to-all(f32[32,12,8,128]{3,2,1,0:T(8,128)S(1)} %get-tuple-element.172), channel_id=1, replica_groups=mesh['ylo'=2,'z'=16,'x'=4,'yhi'=2,'core'=2] {'x','yhi','ylo','core'}, dimensions={0} | all-to-all | bytes 3145728 | tf_op jit(solution)/shard_map/all_to_all | solution.py:393
  169.3 1.5 shard_map.56
  (51 shorter events, 0.9 us)
Async XLA Ops:
  0.0 2.2 %copy-start.4 = (bf16[944,1024]{1,0:T(8,128)(2,1)S(1)}, bf16[944,1024]{1,0:T(8,128)(2,1)}, u32[]{:S(2)}) copy-start(bf16[944,1024]{1,0:T(8,128)(2,1)} %param.10) | copy-start | bytes 5799940
  0.0 2.2 %copy-start.5 = (bf16[944,472]{1,0:T(8,128)(2,1)S(1)}, bf16[944,472]{1,0:T(8,128)(2,1)}, u32[]{:S(2)}) copy-start(bf16[944,472]{1,0:T(8,128)(2,1)} %param.9) | copy-start | bytes 2673412
  5.3 10.8 %copy-start.2 = (s32[1024,8]{0,1:T(8,128)S(1)}, s32[1024,8]{0,1:T(8,128)}, u32[]{:S(2)}) copy-start(s32[1024,8]{0,1:T(8,128)} %param.7) | copy-start | bytes 98308
  5.3 10.8 %copy-start.3 = (s32[1024]{0:T(1024)S(1)}, s32[1024]{0:T(1024)}, u32[]{:S(2)}) copy-start(s32[1024]{0:T(1024)} %param.8) | copy-start | bytes 12292
  5.3 36.2 %all-to-all-start.2 = ((f32[32,14,8,128]{3,2,1,0:T(8,128)}), f32[32,14,8,128]{3,2,1,0:T(8,128)S(1)}, u32[]{:S(2)}, u32[]{:S(2)}) async-start(f32[32,14,8,128]{3,2,1,0:T(8,128)} %shard_map.55), calls=%async_computation.2 | async-start | bytes 3670016 | tf_op jit(solution)/shard_map/all_to_all | solution.py:275
  124.1 10.8 %collective-permute-start = (f32[56,8,128]{2,1,0:T(8,128)S(1)}, f32[56,8,128]{2,1,0:T(8,128)S(1)}, u32[]{:S(2)}, u32[]{:S(2)}) collective-permute-start(f32[56,8,128]{2,1,0:T(8,128)S(1)} %branch_0_fun.5), channel_id=1, source_target_pairs={{0,16},{16,32},{32,48},{48,64},{64,80},{80,96},{96,112},{112,128},... | collective-permute-start | bytes 688136 | tf_op jit(solution)/shard_map/cond/branch_0_fun/ppermute | solution.py:354
  136.6 32.7 %copy-start.1 = (bf16[24,128,1,128]{3,1,2,0:T(8,128)(2,1)S(1)}, bf16[24,128,1,128]{3,1,2,0:T(8,128)(2,1)}, u32[]{:S(2)}) copy-start(bf16[24,128,1,128]{3,1,2,0:T(8,128)(2,1)} %param.11) | copy-start | bytes 2359300
